TPU v7x, 128 devices: a whole 4x4x4 slice. The times are simulated.
128 devices in a mesh: lon: 8 (over z, core), lat: 16 (over x, y).
Axes of the slice: x: 4, y: 4, z: 4, core: 2. Of those that a mesh axis runs over, the one named last changes fastest.
Arguments:
- travel_times: float32 [4096], P(('lon', 'lat')), may hold values from -6 to 6
- ray_counts: int32 [128], P(('lon', 'lat')), may hold values from 4 to 32
- tile_brick: int32 [4096, 4], P(('lon', 'lat')), may hold values from 0 to 127, all different within a row; in each aligned block of 32 rows (0 to 31, 32 to 63, ...) at most 2 rows name the same one
- cell_offsets: int32 [4096, 4, 128], P(('lon', 'lat')), may hold values from 0 to 1023
- cell_depths: int32 [4096, 4, 128], P(('lon', 'lat')), may hold values from 0 to 127
- seg_lengths: float32 [4096, 4, 128], P(('lon', 'lat')), may hold values from 0.002 to 0.02
Outputs:
- model: float32 [256, 512, 128], P('lon', 'lat')
- misfit: float32 [4096], P(('lon', 'lat'))
Inputs may be any that keep to these rules, and one draw needn't show every extreme that they name: `tile_brick`: among the 4 tiles of all rays of one device, no brick is named more than 2 times, a bound that some block reaches; a ray's tiles name different bricks; brick k lives on the device at position k of lon+lat. Only the first ray_counts rays of a device's 32 slots are live.
All inputs are finite; a program needn't handle non-finite values.
Results may differ from a plain program's by a relative error of at most 0.0014.
Values sent between devices are 32-bit elements; how exact they have to be, the bound alone decides.
A program may use at most 64 MiB of HBM per device.

v0:
```python
import jax
import jax.numpy as jnp
from jax import lax
from jax.sharding import Mesh
from jax.sharding import PartitionSpec as P

CLON = 32
CLAT = 32
DEP = 128
ITERS = 2
LON_LAT = ("lon_0", "lon_1", "lat_0", "lat_1")
LON = ("lon_0", "lon_1")
LAT = ("lat_0", "lat_1")


damping = 0.01


def padded(array, sides, width, wrap):
    for axis, dim in sides:
        devices, length = (lax.axis_size(axis), array.shape[dim])
        up = [(i, (i + 1) % devices) for i in range(devices if wrap else devices - 1)]
        down = [(j, i) for i, j in up]
        last = lax.slice_in_dim(array, length - width, length, axis=dim)
        leading = lax.slice_in_dim(array, 0, width, axis=dim)
        before = lax.ppermute(last, axis, up)
        after = lax.ppermute(leading, axis, down)
        array = jnp.concatenate([before, array, after], axis=dim)
    return array


def by_axis(array, axes):
    for axis in axes:
        array = lax.psum(array, axis)
    return array


def shards(travel_times, ray_counts, tile_brick, cell_offsets, cell_depths, seg_lengths):
    devices = lax.axis_size(LON_LAT)
    rays_dev, per_ray, seg_count = cell_offsets.shape
    tiles = rays_dev * per_ray
    slots = 2 * tiles
    capacity = slots // devices
    brick_cells = CLON * CLAT * DEP
    inside = cell_offsets * DEP + cell_depths
    live_mask = (jnp.arange(rays_dev, dtype=jnp.int32) < ray_counts[0]).astype(jnp.float32)
    weights = seg_lengths * live_mask[:, None, None]
    bricks = tile_brick.reshape(tiles)
    onehot = (bricks[:, None] == jnp.arange(devices, dtype=jnp.int32)[None, :]).astype(jnp.int32)
    earlier = jnp.cumsum(onehot, axis=0) - onehot
    rank_in = jnp.sum(earlier * onehot, axis=1)
    slot_index = bricks * capacity + rank_in
    send_offs = (
        jnp.zeros((slots, seg_count), jnp.int32)
        .at[slot_index]
        .set(inside.reshape(tiles, seg_count))
    )
    send_lens = (
        jnp.zeros((slots, seg_count), jnp.float32)
        .at[slot_index]
        .set(weights.reshape(tiles, seg_count))
    )
    held_offs, held_lens = (
        lax.all_to_all(send_offs, LON_LAT, split_axis=0, concat_axis=0, tiled=True),
        lax.all_to_all(send_lens, LON_LAT, split_axis=0, concat_axis=0, tiled=True),
    )

    def forward(grid):
        cells = grid.reshape(brick_cells)
        partial_value = jnp.sum(held_lens * cells[held_offs], axis=1)
        returned = lax.all_to_all(partial_value, LON_LAT, split_axis=0, concat_axis=0, tiled=True)
        return jnp.sum(returned[slot_index].reshape(rays_dev, per_ray), axis=1)

    def backward(ray_vals):
        per_tile = jnp.broadcast_to(ray_vals[:, None], (rays_dev, per_ray)).reshape(tiles)
        slot_vals = jnp.zeros((slots,), jnp.float32).at[slot_index].set(per_tile)
        arrived = lax.all_to_all(slot_vals, LON_LAT, split_axis=0, concat_axis=0, tiled=True)
        terms = held_lens * arrived[:, None]
        cells = (
            jnp.zeros((brick_cells,), jnp.float32).at[held_offs.reshape(-1)].add(terms.reshape(-1))
        )
        return cells.reshape(CLON, CLAT, DEP)

    def smoothing(field):
        lon_pad = padded(field, ((LON, 0),), 1, True)
        lat_pad = padded(field, ((LAT, 1),), 1, False)
        dep_pad = jnp.pad(field, ((0, 0), (0, 0), (1, 1)))
        result = 6.0 * field - lon_pad[2:] - lon_pad[:-2] - lat_pad[:, 2:] - lat_pad[:, :-2]
        return result - dep_pad[:, :, 2:] - dep_pad[:, :, :-2]

    def joint_total(first, second, third, fourth):
        return (
            by_axis(first, LON_LAT),
            by_axis(second, LON_LAT),
            by_axis(third, LON_LAT),
            by_axis(fourth, LON_LAT),
        )

    data = travel_times * live_mask
    u_grid = jnp.zeros((CLON, CLAT, DEP), jnp.float32)
    q_dir = backward(data)
    squares, q_squares, unused_a, unused_b = joint_total(
        jnp.sum(data * data), jnp.sum(q_dir * q_dir), jnp.float32(0.0), jnp.float32(0.0)
    )
    beta_now = jnp.sqrt(squares)
    alpha_now = jnp.sqrt(q_squares) / beta_now
    u_ray = data / beta_now
    v_dir = q_dir / (beta_now * alpha_now)
    search = v_dir
    model = jnp.zeros_like(v_dir)
    phi_bar = beta_now
    rho_bar = alpha_now
    for turn_index in range(ITERS):
        p_ray = forward(v_dir) - alpha_now * u_ray
        p_grid = damping * smoothing(v_dir) - alpha_now * u_grid
        q_dir = backward(p_ray) + damping * smoothing(p_grid)
        squares, q_squares, q_cross, v_squares = joint_total(
            jnp.sum(p_ray * p_ray) + jnp.sum(p_grid * p_grid),
            jnp.sum(q_dir * q_dir),
            jnp.sum(q_dir * v_dir),
            jnp.sum(v_dir * v_dir),
        )
        beta_now = jnp.sqrt(squares)
        alpha_now = jnp.sqrt(q_squares / squares - 2.0 * q_cross + squares * v_squares)
        u_ray = p_ray / beta_now
        u_grid = p_grid / beta_now
        v_dir = (q_dir / beta_now - beta_now * v_dir) / alpha_now
        rho_new = jnp.sqrt(rho_bar * rho_bar + beta_now * beta_now)
        cosine = rho_bar / rho_new
        sine_val = beta_now / rho_new
        theta_val = sine_val * alpha_now
        rho_bar = -cosine * alpha_now
        phi_val = cosine * phi_bar
        phi_bar = sine_val * phi_bar
        model = model + phi_val / rho_new * search
        search = v_dir - theta_val / rho_new * search
    misfit = data - forward(model)
    return (model, misfit)


def solution(mesh):
    torus = Mesh(mesh.devices.reshape(4, 2, 4, 4), ("lon_0", "lon_1", "lat_0", "lat_1"))
    in_specs = (
        P(LON_LAT),
        P(LON_LAT),
        P(LON_LAT, None),
        P(LON_LAT, None, None),
        P(LON_LAT, None, None),
        P(LON_LAT, None, None),
    )
    out_specs = (P(LON, LAT, None), P(LON_LAT))
    return jax.shard_map(
        shards, mesh=torus, in_specs=in_specs, out_specs=out_specs, check_vma=False
    )
```

profile of v0, /device:TPU:1, one launch (start us, length us, event | category | flops | bytes accessed | tf_op | source)
XLA Modules:
  0.0 1198.2 jit_solution(2853526407216503963)
XLA Ops:
  6.1 11.5 all-to-all-start.2
  19.1 8.0 all-to-all-done.2
  34.7 7.1 all-to-all-done
  46.2 9.9 all-to-all-done.1
  56.2 198.7 %scatter_custom_fusion.3 = f32[131072]{0:T(1024)S(1)} fusion(s32[32768]{0:T(1024)S(1)} %bitcast.65, f32[32768]{0:T(1024)S(1)} %bitcast_multiply_fusion.1, f32[]{:T(128)} %constant.9.clone.1), kind=kCustom, calls=%fused_computation.68 | custom fusion | flops 32768 | bytes 524292 | tf_op jit(solution)/shard_map/scatter-add | solution.py:80
  255.6 7.1 all-reduce.8
  262.8 9.6 all-reduce.10
  272.4 7.0 all-reduce.6
  279.4 7.6 all-reduce.4
  289.2 180.5 %gather_fusion = f32[32768]{0:T(1024)S(1)} fusion(f32[131072]{0:T(1024)S(1)} %get-tuple-element.29, s32[32768]{0:T(1024)S(1)} %fusion.31), kind=kCustom, calls=%fused_computation | custom fusion | bytes 393216 | tf_op jit(solution)/shard_map/gather | solution.py:70
  470.8 7.8 all-to-all-start.3
  493.2 10.2 all-to-all-start.4
  503.4 9.5 all-to-all-done.4
  522.0 198.9 %scatter_custom_fusion.5 = f32[131072]{0:T(1024)S(1)} fusion(s32[32768]{0:T(1024)S(1)} %bitcast.66, f32[32768]{0:T(1024)S(1)} %bitcast_multiply_fusion, f32[]{:T(128)} %constant.9.clone.1), kind=kCustom, calls=%fused_computation.66 | custom fusion | flops 32768 | bytes 524292 | tf_op jit(solution)/shard_map/scatter-add | solution.py:80
  723.2 8.5 all-reduce.7
  731.7 8.0 all-reduce.9
  739.7 7.6 all-reduce.5
  747.3 8.9 all-reduce.3
  760.1 180.5 %gather_fusion.2 = f32[32768]{0:T(1024)S(1)} fusion(f32[131072]{0:T(1024)S(1)} %bitcast.55, s32[32768]{0:T(1024)S(1)} %fusion.31), kind=kCustom, calls=%fused_computation.2 | custom fusion | bytes 393216 | tf_op jit(solution)/shard_map/gather | solution.py:70
  941.7 7.5 all-to-all-start.5
  964.4 8.8 psum.220
  977.4 11.9 psum.222
  996.9 180.5 %gather_fusion.4 = f32[32768]{0:T(1024)S(1)} fusion(f32[131072]{0:T(1024)S(1)} %bitcast.56, s32[32768]{0:T(1024)S(1)} %fusion.31), kind=kCustom, calls=%fused_computation.4 | custom fusion | bytes 393216 | tf_op jit(solution)/shard_map/gather | solution.py:70
  1177.8 17.4 %all_to_all.78 = f32[128,2,1]{1,2,0:T(1,128)S(1)} all-to-all(f32[128,2,1]{1,2,0:T(1,128)S(1)} %copy.32), channel_id=1, replica_groups=mesh['lon_0'=4,'lon_1'=2,'lat_0'=4,'lat_1'=4] {'lon_0','lon_1','lat_0','..., dimensions={0} | all-to-all | bytes 2048 | tf_op jit(solution)/shard_map/all_to_all | solution.py:71
  (115 shorter events, 74.3 us)
Async XLA Ops:
  0.6 0.8 copy-start.4
  2.3 0.7 copy-start.5
  6.1 11.5 copy-start.1
  6.1 11.5 copy-start.2
  6.1 21.1 %all-to-all-start.2 = ((f32[128,2,1]{1,2,0:T(1,128)}), f32[128,2,1]{1,2,0:T(1,128)S(1)}, u32[]{:S(2)}, u32[]{:S(2)}) async-start(f32[128,2,1]{1,2,0:T(1,128)} %bitcast.10), calls=%async_computation.2 | async-start | bytes 131072 | tf_op jit(solution)/shard_map/all_to_all | solution.py:77
  27.2 4.5 copy-start.3
  27.2 14.7 %all-to-all-start = ((s32[128,2,128]{2,1,0:T(2,128)}), s32[128,2,128]{2,1,0:T(2,128)S(1)}, u32[]{:S(2)}, u32[]{:S(2)}) async-start(s32[128,2,128]{2,1,0:T(2,128)} %bitcast.3), calls=%async_computation | async-start | bytes 262144 | tf_op jit(solution)/shard_map/all_to_all | solution.py:64
  41.9 14.2 %all-to-all-start.1 = ((f32[128,2,128]{2,1,0:T(2,128)}), f32[128,2,128]{2,1,0:T(2,128)S(1)}, u32[]{:S(2)}, u32[]{:S(2)}) async-start(f32[128,2,128]{2,1,0:T(2,128)} %bitcast.8), calls=%async_computation.1 | async-start | bytes 262144 | tf_op jit(solution)/shard_map/all_to_all | solution.py:65
  470.8 17.4 %all-to-all-start.3 = ((f32[128,2,1]{1,2,0:T(1,128)}), f32[128,2,1]{1,2,0:T(1,128)S(1)}, u32[]{:S(2)}, u32[]{:S(2)}) async-start(f32[128,2,1]{1,2,0:T(1,128)} %copy.27), calls=%async_computation.3 | async-start | bytes 131072 | tf_op jit(solution)/shard_map/all_to_all | solution.py:71
  478.6 35.2 %collective-permute-start.2 = (f32[32,1,128]{2,1,0:T(1,128)S(1)}, f32[32,1,128]{2,1,0:T(1,128)S(1)}, u32[]{:S(2)}, u32[]{:S(2)}) collective-permute-start(f32[32,1,128]{2,1,0:T(1,128)S(1)} %get-tuple-element.47), channel_id=1, source_target_pairs={{1,0},{2,1},{3,2},{4,3},{5,4},{6,5},{7,6},{8,7},{9,8},{10,9},{11,1... | collective-permute-start | bytes 49160 | tf_op jit(solution)/shard_map/ppermute | solution.py:27
  479.9 34.0 %collective-permute-start.3 = (f32[32,1,128]{2,1,0:T(1,128)S(1)}, f32[32,1,128]{2,1,0:T(1,128)S(1)}, u32[]{:S(2)}, u32[]{:S(2)}) collective-permute-start(f32[32,1,128]{2,1,0:T(1,128)S(1)} %get-tuple-element.48), channel_id=1, source_target_pairs={{0,1},{1,2},{2,3},{3,4},{4,5},{5,6},{6,7},{7,8},{8,9},{9,10},{10,1... | collective-permute-start | bytes 49160 | tf_op jit(solution)/shard_map/ppermute | solution.py:26
  483.9 30.0 %collective-permute-start = (f32[1,32,128]{2,1,0:T(8,128)S(1)}, f32[1,32,128]{2,1,0:T(8,128)S(1)}, u32[]{:S(2)}, u32[]{:S(2)}) collective-permute-start(f32[1,32,128]{2,1,0:T(8,128)S(1)} %get-tuple-element.45), channel_id=1, source_target_pairs={{16,0},{32,16},{48,32},{64,48},{80,64},{96,80},{112,96},{0,112},{1... | collective-permute-start | bytes 49160 | tf_op jit(solution)/shard_map/ppermute | solution.py:27
  485.6 28.2 %collective-permute-start.1 = (f32[1,32,128]{2,1,0:T(8,128)S(1)}, f32[1,32,128]{2,1,0:T(8,128)S(1)}, u32[]{:S(2)}, u32[]{:S(2)}) collective-permute-start(f32[1,32,128]{2,1,0:T(8,128)S(1)} %get-tuple-element.46), channel_id=1, source_target_pairs={{0,16},{16,32},{32,48},{48,64},{64,80},{80,96},{96,112},{112,0},{1... | collective-permute-start | bytes 49160 | tf_op jit(solution)/shard_map/ppermute | solution.py:26
  493.2 19.7 %all-to-all-start.4 = ((f32[128,2,1]{1,2,0:T(1,128)}), f32[128,2,1]{1,2,0:T(1,128)S(1)}, u32[]{:S(2)}, u32[]{:S(2)}) async-start(f32[128,2,1]{1,2,0:T(1,128)} %bitcast.19), calls=%async_computation.4 | async-start | bytes 131072 | tf_op jit(solution)/shard_map/all_to_all | solution.py:77
  514.9 207.3 %collective-permute-start.4 = (f32[1,32,128]{2,1,0:T(8,128)S(1)}, f32[1,32,128]{2,1,0:T(8,128)S(1)}, u32[]{:S(2)}, u32[]{:S(2)}) collective-permute-start(f32[1,32,128]{2,1,0:T(8,128)S(1)} %get-tuple-element.41), channel_id=1, source_target_pairs={{16,0},{32,16},{48,32},{64,48},{80,64},{96,80},{112,96},{0,112},{1... | collective-permute-start | bytes 49160 | tf_op jit(solution)/shard_map/ppermute | solution.py:27
  515.9 206.3 %collective-permute-start.5 = (f32[1,32,128]{2,1,0:T(8,128)S(1)}, f32[1,32,128]{2,1,0:T(8,128)S(1)}, u32[]{:S(2)}, u32[]{:S(2)}) collective-permute-start(f32[1,32,128]{2,1,0:T(8,128)S(1)} %get-tuple-element.42), channel_id=1, source_target_pairs={{0,16},{16,32},{32,48},{48,64},{64,80},{80,96},{96,112},{112,0},{1... | collective-permute-start | bytes 49160 | tf_op jit(solution)/shard_map/ppermute | solution.py:26
  516.6 205.5 %collective-permute-start.6 = (f32[32,1,128]{2,1,0:T(1,128)S(1)}, f32[32,1,128]{2,1,0:T(1,128)S(1)}, u32[]{:S(2)}, u32[]{:S(2)}) collective-permute-start(f32[32,1,128]{2,1,0:T(1,128)S(1)} %get-tuple-element.43), channel_id=1, source_target_pairs={{1,0},{2,1},{3,2},{4,3},{5,4},{6,5},{7,6},{8,7},{9,8},{10,9},{11,1... | collective-permute-start | bytes 49160 | tf_op jit(solution)/shard_map/ppermute | solution.py:27
  517.9 204.2 %collective-permute-start.7 = (f32[32,1,128]{2,1,0:T(1,128)S(1)}, f32[32,1,128]{2,1,0:T(1,128)S(1)}, u32[]{:S(2)}, u32[]{:S(2)}) collective-permute-start(f32[32,1,128]{2,1,0:T(1,128)S(1)} %get-tuple-element.44), channel_id=1, source_target_pairs={{0,1},{1,2},{2,3},{3,4},{4,5},{5,6},{6,7},{7,8},{8,9},{9,10},{10,1... | collective-permute-start | bytes 49160 | tf_op jit(solution)/shard_map/ppermute | solution.py:26
  941.7 17.2 %all-to-all-start.5 = ((f32[128,2,1]{1,2,0:T(1,128)}), f32[128,2,1]{1,2,0:T(1,128)S(1)}, u32[]{:S(2)}, u32[]{:S(2)}) async-start(f32[128,2,1]{1,2,0:T(1,128)} %copy.30), calls=%async_computation.5 | async-start | bytes 131072 | tf_op jit(solution)/shard_map/all_to_all | solution.py:71
  949.4 12.6 %collective-permute-start.8 = (f32[1,32,128]{2,1,0:T(8,128)S(1)}, f32[1,32,128]{2,1,0:T(8,128)S(1)}, u32[]{:S(2)}, u32[]{:S(2)}) collective-permute-start(f32[1,32,128]{2,1,0:T(8,128)S(1)} %get-tuple-element.37), channel_id=1, source_target_pairs={{16,0},{32,16},{48,32},{64,48},{80,64},{96,80},{112,96},{0,112},{1... | collective-permute-start | bytes 49160 | tf_op jit(solution)/shard_map/ppermute | solution.py:27
  950.6 11.3 collective-permute-start.9
  951.3 10.6 collective-permute-start.10
  952.6 9.4 collective-permute-start.11
  996.9 180.6 %copy-start = (f32[32,32,128]{2,1,0:T(8,128)}, f32[32,32,128]{2,1,0:T(8,128)S(1)}, u32[]{:S(2)}) copy-start(f32[32,32,128]{2,1,0:T(8,128)S(1)} %multiply_add_fusion) | copy-start | bytes 1572868
where the time goes:
time: 1200 us
  local copies, waits for them, and re-layouts  557 us (46%)
  other arithmetic  412 us (34%)
  blocking collectives  113 us (9%)
  starting transfers between devices  67.6 us (6%)
  waiting for transfers between devices  38.7 us (3%)
    gather x3, local copies, waits for them, and re-layouts, forward(): partial_value = jnp.sum(held_lens * cells[held_offs], axis=1)  542 us
    scatter-add x2, other arithmetic, backward(): jnp.zeros((brick_cells,), jnp.float32).at[held_offs.reshape(-1)]  398 us
    psum x12, blocking collectives, by_axis(): array = lax.psum(array, axis)  95.8 us
  transfers between devices with their start and end apart: 18, of which 6 were waited for; matrix products, arithmetic and copies ran while one was open for 18% of the time, Pallas kernels for 0%

commit v1 on v0

v1 whole, which is shorter than its diff:
```python
import functools

import jax
import jax.numpy as jnp
from jax import lax
from jax.experimental import pallas as pl
from jax.experimental.pallas import tpu as pltpu
from jax.sharding import Mesh
from jax.sharding import PartitionSpec as P

CLON, CLAT, DEP, SEG = 32, 32, 128, 128
COLS = CLON * CLAT
RAYS, TPR = 32, 4
NDEV = 128
SLOTS = 2 * NDEV
CHUNK = 8
SCALE = 8.0
DAMP = 0.01 * SCALE
LON_LAT = ("lon_0", "lon_1", "lat_0", "lat_1")
LON = ("lon_0", "lon_1")
LAT = ("lat_0", "lat_1")

f32, bf16, i32 = jnp.float32, jnp.bfloat16, jnp.int32
VMEM = pl.BlockSpec(memory_space=pltpu.VMEM)
SMEM = pl.BlockSpec(memory_space=pltpu.SMEM)
PARAMS = pltpu.CompilerParams(vmem_limit_bytes=48 << 20)


def iota(shape, dim):
    return lax.broadcasted_iota(i32, shape, dim)


def split2(x):
    hi = x.astype(bf16)
    return hi, (x - hi.astype(f32)).astype(bf16)


def split3(x):
    hi = x.astype(bf16)
    rest = x - hi.astype(f32)
    mid = rest.astype(bf16)
    return hi, mid, (rest - mid.astype(f32)).astype(bf16)


def as_payload(cell, lens):
    col = cell >> 7
    parts = [(cell & 127), (col & 127), (col >> 7)]
    return jnp.concatenate([p.astype(f32).astype(bf16) for p in parts] + list(split3(lens)), axis=1)


def from_payload(rows):
    z, low, high, hi, mid, lo = [rows[:, k * 128:(k + 1) * 128] for k in range(6)]
    return z, high * 128.0 + low, (hi + mid) + lo


def pack_kernel(count, brick, times, offs, deps, lens, out, pay):
    lane = iota((RAYS, 128), 1)
    mine = iota((RAYS, 128), 0) == (lane & 31)
    tb = brick[...]
    wide = jnp.zeros((RAYS, 128), i32)
    for k in range(TPR):
        wide = jnp.where((lane >> 5) == k, tb[:, k:k + 1], wide)
    brick_row = jnp.sum(jnp.where(mine, wide, 0).astype(f32), axis=0, keepdims=True)
    time_row = jnp.concatenate([times[...]] * TPR, axis=1)
    ray_row = iota((1, 128), 1) & 31
    live = ray_row < count[0]
    as_rows = jnp.broadcast_to(brick_row, (128, 128))
    same = (as_rows == as_rows.T) & (iota((128, 128), 0) < iota((128, 128), 1))
    rank_row = jnp.sum(jnp.where(same, 1.0, 0.0), axis=0, keepdims=True)
    for k in range(TPR):
        cell = offs[:, k, :] * DEP + deps[:, k, :]
        pay[k * RAYS:(k + 1) * RAYS, :] = as_payload(cell, lens[:, k, :] * SCALE)
    target = iota((128, 128), 0).astype(f32)
    meta = jnp.zeros((128, 128), f32)
    lanes = iota((128, 128), 1)
    for k in range(2):
        picked = jnp.where((target == brick_row) & (rank_row == k) & live, 1.0, 0.0)
        z, col, w = from_payload(jnp.dot(picked.astype(bf16), pay[...], preferred_element_type=f32))
        out[:, k, :] = col * 128.0 + z
        out[:, 2 + k, :] = w
        value = jnp.sum(picked * time_row, axis=1, keepdims=True)
        ray = jnp.sum(picked * (ray_row + 1).astype(f32), axis=1, keepdims=True)
        meta = jnp.where(lanes == k, value, jnp.where(lanes == 2 + k, ray, meta))
    out[:, 4, :] = meta


def onehot_cols(col_row):
    at = jnp.broadcast_to(col_row.astype(jnp.int16), (COLS, 128))
    return jnp.where(lax.broadcasted_iota(jnp.int16, (COLS, 128), 0) == at, jnp.ones((), bf16), jnp.zeros((), bf16))


def scatter_into(acc, n, col, dep, wy, oht, vt):
    acc[...] = jnp.zeros_like(acc)

    def body(c, carry):
        for j in range(CHUNK):
            row = pl.ds(c * CHUNK + j, 1)
            at = slice(j * 128, (j + 1) * 128)
            oht[:, at] = onehot_cols(col[row, :])
            w = wy[row, :]
            hi = w.astype(bf16).astype(f32)
            here = iota((DEP, 128), 0) == dep[row, :]
            vt[0:128, at] = jnp.where(here, hi, 0.0).astype(bf16)
            vt[128:256, at] = jnp.where(here, w - hi, 0.0).astype(bf16)
        acc[...] += lax.dot_general(oht[...], vt[...], (((1,), (1,)), ((), ())), preferred_element_type=f32)
        return carry

    lax.fori_loop(0, (n + CHUNK - 1) // CHUNK, body, 0)


def gather_from(grid, n, col, dep, w, out, oht, gt):
    hi, lo = split2(grid.T)
    gt[0:128, :] = hi
    gt[128:256, :] = lo
    out[...] = jnp.zeros_like(out)

    def body(c, carry):
        for j in range(CHUNK):
            oht[:, j * 128:(j + 1) * 128] = onehot_cols(col[pl.ds(c * CHUNK + j, 1), :])
        res = jnp.dot(gt[...], oht[...], preferred_element_type=f32)
        for j in range(CHUNK):
            row = pl.ds(c * CHUNK + j, 1)
            at = slice(j * 128, (j + 1) * 128)
            both = res[0:128, at] + res[128:256, at]
            here = iota((DEP, 128), 0) == dep[row, :]
            out[row, :] = jnp.sum(jnp.where(here, both, 0.0), axis=0, keepdims=True) * w[row, :]
        return carry

    lax.fori_loop(0, (n + CHUNK - 1) // CHUNK, body, 0)


def place_of(slot_info):
    return jnp.where(iota((SLOTS, SLOTS), 0) == slot_info, 1.0, 0.0)


def to_rays(partial, place, rays):
    row = jnp.sum(place * partial, axis=0, keepdims=True)
    total = jnp.zeros((RAYS, NDEV), f32)
    for k in range(2):
        at = slice(k * 128, (k + 1) * 128)
        total += jnp.where(iota((RAYS, NDEV), 0) == rays[:, at], row[:, at], 0.0)
    return total


def from_rays(values, place, rays):
    rows = [
        jnp.sum(jnp.where(iota((RAYS, NDEV), 0) == rays[:, k * 128:(k + 1) * 128], values, 0.0), axis=0, keepdims=True)
        for k in range(2)
    ]
    return jnp.sum(place * jnp.concatenate(rows, axis=1), axis=1, keepdims=True)


def first_kernel(held, q_out, p_out, col, dep, w, info, count, oht, vt, acc, gt, wy):
    meta = held[:, 4, :].T
    y_row = jnp.concatenate([meta[0:1, :], meta[1:2, :]], axis=1)
    ray_row = jnp.concatenate([meta[2:3, :], meta[3:4, :]], axis=1).astype(i32) - 1
    live = ray_row >= 0
    flags = jnp.broadcast_to(jnp.where(live, 1.0, 0.0), (8, SLOTS)).astype(bf16)
    before = jnp.where(iota((SLOTS, SLOTS), 0) < iota((SLOTS, SLOTS), 1), 1.0, 0.0).astype(bf16)
    at = jnp.dot(flags, before, preferred_element_type=f32)[0:1, :].astype(i32)
    at = jnp.where(live, at, -1)
    info[0:1, :] = at
    info[1:2, :] = ray_row
    n = jnp.sum(jnp.where(live, 1.0, 0.0)).astype(i32)
    count[0] = n
    place = place_of(at)
    pay = jnp.concatenate([as_payload(held[:, k, :].astype(i32), held[:, 2 + k, :]) for k in range(2)], axis=0)
    z, c, lens = from_payload(jnp.dot(place.astype(bf16), pay, preferred_element_type=f32))
    col[...] = c.astype(i32)
    dep[...] = z.astype(i32)
    w[...] = lens
    wy[...] = lens * jnp.sum(place * y_row, axis=1, keepdims=True)
    scatter_into(acc, n, col, dep, wy, oht, vt)
    q = acc[:, 0:128] + acc[:, 128:256]
    q_out[...] = q
    gather_from(q, n, col, dep, w, wy, oht, gt)
    p_out[...] = to_rays(jnp.sum(wy[...], axis=1, keepdims=True), place, ray_row)


def second_kernel(p, smooth, col, dep, w, info, count, q_out, p_out, oht, vt, acc, gt, wy):
    n = count[0]
    place = place_of(info[0:1, :])
    ray_row = info[1:2, :]
    wy[...] = w[...] * from_rays(p[...], place, ray_row)
    scatter_into(acc, n, col, dep, wy, oht, vt)
    q = acc[:, 0:128] + acc[:, 128:256] + smooth[...]
    q_out[...] = q
    gather_from(q, n, col, dep, w, wy, oht, gt)
    p_out[...] = to_rays(jnp.sum(wy[...], axis=1, keepdims=True), place, ray_row)


def shape(dims, dtype=f32):
    return jax.ShapeDtypeStruct(dims, dtype)


SCRATCH = [
    pltpu.VMEM((COLS, CHUNK * 128), bf16),
    pltpu.VMEM((256, CHUNK * 128), bf16),
    pltpu.VMEM((COLS, 256), f32),
    pltpu.VMEM((256, COLS), bf16),
    pltpu.VMEM((SLOTS, SEG), f32),
]


def padded(array, sides, width, wrap):
    for axis, dim in sides:
        devices, length = (lax.axis_size(axis), array.shape[dim])
        up = [(i, (i + 1) % devices) for i in range(devices if wrap else devices - 1)]
        down = [(j, i) for i, j in up]
        last = lax.slice_in_dim(array, length - width, length, axis=dim)
        leading = lax.slice_in_dim(array, 0, width, axis=dim)
        before = lax.ppermute(last, axis, up)
        after = lax.ppermute(leading, axis, down)
        array = jnp.concatenate([before, array, after], axis=dim)
    return array


def smoothing(flat):
    field = flat.reshape(CLON, CLAT, DEP)
    lon_pad = padded(field, ((LON, 0),), 1, True)
    lat_pad = padded(field, ((LAT, 1),), 1, False)
    dep_pad = jnp.pad(field, ((0, 0), (0, 0), (1, 1)))
    result = 6.0 * field - lon_pad[2:] - lon_pad[:-2] - lat_pad[:, 2:] - lat_pad[:, :-2]
    return (result - dep_pad[:, :, 2:] - dep_pad[:, :, :-2]).reshape(COLS, DEP)


def shards(travel_times, ray_counts, tile_brick, cell_offsets, cell_depths, seg_lengths):
    live_mask = (jnp.arange(RAYS, dtype=i32) < ray_counts[0]).astype(f32)
    send = pl.pallas_call(
        pack_kernel,
        out_shape=shape((NDEV, 5, SEG)),
        in_specs=[SMEM] + [VMEM] * 5,
        out_specs=VMEM,
        scratch_shapes=[pltpu.VMEM((128, 768), bf16)],
        compiler_params=PARAMS,
    )(ray_counts, tile_brick, travel_times.reshape(1, RAYS), cell_offsets, cell_depths, seg_lengths)
    held = lax.all_to_all(send, LON_LAT, split_axis=0, concat_axis=0, tiled=True)
    q0, p_part, col, dep, w, info, count = pl.pallas_call(
        first_kernel,
        out_shape=(shape((COLS, DEP)), shape((RAYS, NDEV)), shape((SLOTS, SEG), i32), shape((SLOTS, SEG), i32),
                   shape((SLOTS, SEG)), shape((2, SLOTS), i32), shape((1,), i32)),
        in_specs=[VMEM],
        out_specs=(VMEM,) * 6 + (SMEM,),
        scratch_shapes=SCRATCH,
        compiler_params=PARAMS,
    )(held)
    p0 = lax.psum(p_part, LON_LAT)
    g0 = DAMP * smoothing(q0)
    smooth = DAMP * smoothing(g0)
    q1, p_part = pl.pallas_call(
        second_kernel,
        out_shape=(shape((COLS, DEP)), shape((RAYS, NDEV))),
        in_specs=[VMEM] * 6 + [SMEM],
        out_specs=(VMEM,) * 2,
        scratch_shapes=SCRATCH,
        compiler_params=PARAMS,
    )(p0, smooth, col, dep, w, info, count)
    g1 = DAMP * smoothing(q1)
    dots = jnp.stack([jnp.sum(q0 * q0), jnp.sum(g0 * g0), jnp.sum(q1 * q1), jnp.sum(g1 * g1)])
    row = jnp.concatenate([dots, jnp.zeros((NDEV - 4,), f32)])
    both = lax.psum(jnp.concatenate([p_part, row[None, :]], axis=0), LON_LAT)
    p1 = both[:RAYS]
    m0 = both[RAYS, 0]
    m1 = both[RAYS, 1] + jnp.sum(p0 * p0)
    m2 = both[RAYS, 2]
    m3 = both[RAYS, 3] + jnp.sum(p1 * p1)
    r1, r2, r3 = m1 / m0, m2 / m1, m3 / m2
    c0 = (r3 - r1) / (r3 - r2) / r1
    c1 = (r1 - r2) / (r3 - r2) / (r1 * r2)
    model = SCALE * (c0 * q0 + c1 * q1)
    me = lax.axis_index(LON_LAT)
    mine = lambda p: lax.dynamic_slice_in_dim(p, me, 1, axis=1)[:, 0]
    misfit = travel_times * live_mask - c0 * mine(p0) - c1 * mine(p1)
    return (model.reshape(CLON, CLAT, DEP), misfit)


def solution(mesh):
    torus = Mesh(mesh.devices.reshape(4, 2, 4, 4), LON_LAT)
    in_specs = (
        P(LON_LAT),
        P(LON_LAT),
        P(LON_LAT, None),
        P(LON_LAT, None, None),
        P(LON_LAT, None, None),
        P(LON_LAT, None, None),
    )
    out_specs = (P(LON, LAT, None), P(LON_LAT))
    return jax.shard_map(shards, mesh=torus, in_specs=in_specs, out_specs=out_specs, check_vma=False)
```

time: 1200 us -> 273 us (0.23)
  local copies, waits for them, and re-layouts: 557 us -> 7.29 us
  other arithmetic: 412 us -> 6.79 us
  Pallas kernels: 0 us -> 36 us
  waiting for transfers between devices: 38.7 us -> 14 us
  blocking collectives: 113 us -> 135 us
    gather x6 -> x0, local copies, waits for them, and re-layouts: 545 us -> none  [the longest x3 542 us: forward(): partial_value = jnp.sum(held_lens * cells[held_offs], axis=1)]
    scatter-add x2 -> x0, other arithmetic: 398 us -> none  [backward(): jnp.zeros((brick_cells,), jnp.float32).at[held_offs.reshape(-1)]]
    psum x12 -> x2, blocking collectives: 95.8 us -> 135 us  [the longest x1 69.6 us: shards(): both = lax.psum(jnp.concatenate([p_part, row[None, :]], axis=0), LON_LAT)]
    pallas_call x0 -> x3, Pallas kernels: none -> 36 us  [the longest x1 17.6 us: shards(): pl.pallas_call(first_kernel, out_shape=(shape((COLS, DEP)), shape((RAYS,...]
    all_to_all x6 -> x1, starting transfers between devices: 45.6 us -> 11.5 us  [shards(): lax.all_to_all(send, LON_LAT, split_axis=0, concat_axis=0, tiled=True)]
    ppermute x6, starting transfers between devices: 7.84 us -> 40.7 us  [padded(): after = lax.ppermute(leading, axis, down)]
    all_to_all x6 -> x1, waiting for transfers between devices: 38.7 us -> 13.3 us  [shards(): lax.all_to_all(send, LON_LAT, split_axis=0, concat_axis=0, tiled=True)]
    all_to_all x1 -> x0, blocking collectives: 17.4 us -> none  [forward(): lax.all_to_all(partial_value, LON_LAT, split_axis=0, concat_axis=0, tiled...]
  transfers between devices with their start and end apart: 18 -> 13, of which waited for: 6 -> 4; matrix products, arithmetic and copies ran while one was open for 18% -> 1% of each run, Pallas kernels for 0% -> 0%
where the time goes in v1:
time: 273 us; the launch traced here: 272 us
  blocking collectives  135 us (49%)
  starting transfers between devices  66.1 us (24%)
  Pallas kernels  36 us (13%)
  waiting for transfers between devices  14 us (5%)
  local copies, waits for them, and re-layouts  7.29 us (3%)
  other arithmetic  6.79 us (2%)
  between operations  6.66 us (2%)
    psum x1, blocking collectives, shards(): both = lax.psum(jnp.concatenate([p_part, row[None, :]], axis=0), LON_LAT)  69.6 us
    psum x1, blocking collectives, shards(): p0 = lax.psum(p_part, LON_LAT)  65.7 us
    ppermute x6, starting transfers between devices, padded(): after = lax.ppermute(leading, axis, down)  40.7 us
    pallas_call x1, Pallas kernels, shards(): pl.pallas_call(first_kernel, out_shape=(shape((COLS, DEP)), shape((RAYS,...  17.6 us
    pallas_call x1, Pallas kernels, shards(): pl.pallas_call(second_kernel, out_shape=(shape((COLS, DEP)), shape((RAYS,...  16.5 us
    ppermute x6, starting transfers between devices, padded(): before = lax.ppermute(last, axis, up)  13.9 us
    all_to_all x1, waiting for transfers between devices, shards(): lax.all_to_all(send, LON_LAT, split_axis=0, concat_axis=0, tiled=True)  13.3 us
    all_to_all x1, starting transfers between devices, shards(): lax.all_to_all(send, LON_LAT, split_axis=0, concat_axis=0, tiled=True)  11.5 us
  transfers between devices with their start and end apart: 13, of which 4 were waited for; matrix products, arithmetic and copies ran while one was open for 1% of the time, Pallas kernels for 0%

profile of v1, /device:TPU:1, one launch (start us, length us, event | category | flops | bytes accessed | tf_op | source)
XLA Modules:
  0.0 272.1 jit_solution(8706282119575643636)
XLA Ops:
  2.7 0.8 copy-done
  3.5 0.8 copy-done.1
  4.4 0.8 copy-done.2
  5.2 1.9 shard_map.77
  7.1 11.5 %all-to-all-start = ((f32[128,5,128]{2,1,0:T(8,128)}), f32[128,5,128]{2,1,0:T(8,128)S(1)}, u32[]{:S(2)}, u32[]{:S(2)}) async-start(f32[128,5,128]{2,1,0:T(8,128)} %shard_map.77), calls=%async_computation | async-start | bytes 1048576 | tf_op jit(solution)/shard_map/all_to_all | solution.py:237
  18.6 13.3 %all-to-all-done.held = f32[128,5,128]{2,1,0:T(8,128)S(1)} async-done(((f32[128,5,128]{2,1,0:T(8,128)}), f32[128,5,128]{2,1,0:T(8,128)S(1)}, u32[]{:S(2)}, u32[]{:S(2)}) %all-to-all-start) | async-done | bytes 327712 | tf_op jit(solution)/shard_map/all_to_all | solution.py:237
  31.9 17.6 %shard_map.78 = (f32[1024,128]{1,0:T(8,128)S(1)}, f32[32,128]{1,0:T(8,128)S(1)}, s32[256,128]{1,0:T(8,128)S(1)}, s32[256,128]{1,0:T(8,128)S(1)}, f32[256,128]{1,...) custom-call(f32[128,5,128]{2,1,0:T(8,128)S(1)} %all-to-all-done.held), custom_call_target="tpu_custom_call" | custom-call | tf_op jit(solution)/shard_map/pallas_call | solution.py:238
  49.6 1.3 collective-permute-start.2
  50.9 4.0 %collective-permute-start.3 = (f32[32,1,128]{2,1,0:T(1,128)S(1)}, f32[32,1,128]{2,1,0:T(1,128)S(1)}, u32[]{:S(2)}, u32[]{:S(2)}) collective-permute-start(f32[32,1,128]{2,1,0:T(1,128)S(1)} %get-tuple-element.33), channel_id=1, source_target_pairs={{0,1},{1,2},{2,3},{3,4},{4,5},{5,6},{6,7},{7,8},{8,9},{9,10},{10,1... | collective-permute-start | bytes 49160 | tf_op jit(solution)/shard_map/ppermute | solution.py:212
  54.9 17.6 %collective-permute-start = (f32[1,32,128]{2,1,0:T(8,128)S(1)}, f32[1,32,128]{2,1,0:T(8,128)S(1)}, u32[]{:S(2)}, u32[]{:S(2)}) collective-permute-start(f32[1,32,128]{2,1,0:T(8,128)S(1)} %get-tuple-element.30), channel_id=1, source_target_pairs={{16,0},{32,16},{48,32},{64,48},{80,64},{96,80},{112,96},{0,112},{1... | collective-permute-start | bytes 49160 | tf_op jit(solution)/shard_map/ppermute | solution.py:213
  72.5 0.8 multiply_reduce_fusion.2
  73.3 65.7 %psum.14.p = f32[32,128]{1,0:T(8,128)S(1)} all-reduce(f32[32,128]{1,0:T(8,128)S(1)} %get-tuple-element.11), channel_id=1, replica_groups=mesh['lon_0'=4,'lon_1'=2,'lat_0'=4,'lat_1'=4] {'lon_0','lon_1','lat_0','..., use_global_device_ids=true, to_apply=%region_0.0 | all-reduce | flops 4096 | bytes 32768 | tf_op jit(solution)/shard_map/psum | solution.py:247
  139.0 1.0 multiply_reduce_fusion.1
  140.7 2.0 collective-permute-start.5
  142.7 1.3 collective-permute-start.6
  144.0 4.0 %collective-permute-start.7 = (f32[32,1,128]{2,1,0:T(1,128)S(1)}, f32[32,1,128]{2,1,0:T(1,128)S(1)}, u32[]{:S(2)}, u32[]{:S(2)}) collective-permute-start(f32[32,1,128]{2,1,0:T(1,128)S(1)} %get-tuple-element.29), channel_id=1, source_target_pairs={{0,1},{1,2},{2,3},{3,4},{4,5},{5,6},{6,7},{7,8},{8,9},{9,10},{10,1... | collective-permute-start | bytes 49160 | tf_op jit(solution)/shard_map/ppermute | solution.py:212
  149.2 16.5 %shard_map.79 = (f32[1024,128]{1,0:T(8,128)S(1)}, f32[32,128]{1,0:T(8,128)S(1)}) custom-call(f32[32,128]{1,0:T(8,128)S(1)} %psum.14.p, f32[1024,128]{1,0:T(8,128)S(1)} %bitcast.28, s32[256,128]{1,0:T(8,128)S(1)} %get-tuple-element.13.col, s32[256,128]{1,0:T(8,128)S(1)} %get-tuple-element.14.dep, f32[256,128]{1,0:T(8,128)S(1)} %get-tuple-element.15.w, ...), custom_call_target="tpu_custom_call" | custom-call | tf_op jit(solution)/shard_map/pallas_call | solution.py:250
  165.7 1.3 collective-permute-start.10
  167.0 4.0 %collective-permute-start.11 = (f32[32,1,128]{2,1,0:T(1,128)S(1)}, f32[32,1,128]{2,1,0:T(1,128)S(1)}, u32[]{:S(2)}, u32[]{:S(2)}) collective-permute-start(f32[32,1,128]{2,1,0:T(1,128)S(1)} %get-tuple-element.25), channel_id=1, source_target_pairs={{0,1},{1,2},{2,3},{3,4},{4,5},{5,6},{6,7},{7,8},{8,9},{9,10},{10,1... | collective-permute-start | bytes 49160 | tf_op jit(solution)/shard_map/ppermute | solution.py:212
  171.0 18.6 %collective-permute-start.8 = (f32[1,32,128]{2,1,0:T(8,128)S(1)}, f32[1,32,128]{2,1,0:T(8,128)S(1)}, u32[]{:S(2)}, u32[]{:S(2)}) collective-permute-start(f32[1,32,128]{2,1,0:T(8,128)S(1)} %get-tuple-element.22), channel_id=1, source_target_pairs={{16,0},{32,16},{48,32},{64,48},{80,64},{96,80},{112,96},{0,112},{1... | collective-permute-start | bytes 49160 | tf_op jit(solution)/shard_map/ppermute | solution.py:213
  190.8 1.0 fusion.9
  191.8 2.6 concatenate.60
  194.5 69.6 %psum.15 = f32[33,128]{1,0:T(8,128)S(1)} all-reduce(f32[33,128]{1,0:T(8,128)S(1)} %pad_maximum_fusion.12), channel_id=1, replica_groups=mesh['lon_0'=4,'lon_1'=2,'lat_0'=4,'lat_1'=4] {'lon_0','lon_1','lat_0','..., use_global_device_ids=true, to_apply=%region_5.6 | all-reduce | flops 4224 | bytes 33792 | tf_op jit(solution)/shard_map/psum | solution.py:261
  270.5 0.9 add_multiply_fusion
  (37 shorter events, 6.6 us)
Async XLA Ops:
  2.0 0.7 copy-start.3
  2.7 0.8 copy-start
  3.5 0.8 copy-start.1
  4.4 0.8 copy-start.2
  7.1 24.8 %all-to-all-start = ((f32[128,5,128]{2,1,0:T(8,128)}), f32[128,5,128]{2,1,0:T(8,128)S(1)}, u32[]{:S(2)}, u32[]{:S(2)}) async-start(f32[128,5,128]{2,1,0:T(8,128)} %shard_map.77), calls=%async_computation | async-start | bytes 1048576 | tf_op jit(solution)/shard_map/all_to_all | solution.py:237
  49.6 89.4 %collective-permute-start.2 = (f32[32,1,128]{2,1,0:T(1,128)S(1)}, f32[32,1,128]{2,1,0:T(1,128)S(1)}, u32[]{:S(2)}, u32[]{:S(2)}) collective-permute-start(f32[32,1,128]{2,1,0:T(1,128)S(1)} %get-tuple-element.32), channel_id=1, source_target_pairs={{1,0},{2,1},{3,2},{4,3},{5,4},{6,5},{7,6},{8,7},{9,8},{10,9},{11,1... | collective-permute-start | bytes 49160 | tf_op jit(solution)/shard_map/ppermute | solution.py:213
  50.9 88.1 %collective-permute-start.3 = (f32[32,1,128]{2,1,0:T(1,128)S(1)}, f32[32,1,128]{2,1,0:T(1,128)S(1)}, u32[]{:S(2)}, u32[]{:S(2)}) collective-permute-start(f32[32,1,128]{2,1,0:T(1,128)S(1)} %get-tuple-element.33), channel_id=1, source_target_pairs={{0,1},{1,2},{2,3},{3,4},{4,5},{5,6},{6,7},{7,8},{8,9},{9,10},{10,1... | collective-permute-start | bytes 49160 | tf_op jit(solution)/shard_map/ppermute | solution.py:212
  54.9 84.1 %collective-permute-start = (f32[1,32,128]{2,1,0:T(8,128)S(1)}, f32[1,32,128]{2,1,0:T(8,128)S(1)}, u32[]{:S(2)}, u32[]{:S(2)}) collective-permute-start(f32[1,32,128]{2,1,0:T(8,128)S(1)} %get-tuple-element.30), channel_id=1, source_target_pairs={{16,0},{32,16},{48,32},{64,48},{80,64},{96,80},{112,96},{0,112},{1... | collective-permute-start | bytes 49160 | tf_op jit(solution)/shard_map/ppermute | solution.py:213
  72.5 66.5 %collective-permute-start.1 = (f32[1,32,128]{2,1,0:T(8,128)S(1)}, f32[1,32,128]{2,1,0:T(8,128)S(1)}, u32[]{:S(2)}, u32[]{:S(2)}) collective-permute-start(f32[1,32,128]{2,1,0:T(8,128)S(1)} %get-tuple-element.31), channel_id=1, source_target_pairs={{0,16},{16,32},{32,48},{48,64},{64,80},{80,96},{96,112},{112,0},{1... | collective-permute-start | bytes 49160 | tf_op jit(solution)/shard_map/ppermute | solution.py:212
  140.1 8.5 %collective-permute-start.4 = (f32[1,32,128]{2,1,0:T(8,128)S(1)}, f32[1,32,128]{2,1,0:T(8,128)S(1)}, u32[]{:S(2)}, u32[]{:S(2)}) collective-permute-start(f32[1,32,128]{2,1,0:T(8,128)S(1)} %get-tuple-element.26), channel_id=1, source_target_pairs={{16,0},{32,16},{48,32},{64,48},{80,64},{96,80},{112,96},{0,112},{1... | collective-permute-start | bytes 49160 | tf_op jit(solution)/shard_map/ppermute | solution.py:213
  140.7 7.9 %collective-permute-start.5 = (f32[1,32,128]{2,1,0:T(8,128)S(1)}, f32[1,32,128]{2,1,0:T(8,128)S(1)}, u32[]{:S(2)}, u32[]{:S(2)}) collective-permute-start(f32[1,32,128]{2,1,0:T(8,128)S(1)} %get-tuple-element.27), channel_id=1, source_target_pairs={{0,16},{16,32},{32,48},{48,64},{64,80},{80,96},{96,112},{112,0},{1... | collective-permute-start | bytes 49160 | tf_op jit(solution)/shard_map/ppermute | solution.py:212
  142.7 5.9 %collective-permute-start.6 = (f32[32,1,128]{2,1,0:T(1,128)S(1)}, f32[32,1,128]{2,1,0:T(1,128)S(1)}, u32[]{:S(2)}, u32[]{:S(2)}) collective-permute-start(f32[32,1,128]{2,1,0:T(1,128)S(1)} %get-tuple-element.28), channel_id=1, source_target_pairs={{1,0},{2,1},{3,2},{4,3},{5,4},{6,5},{7,6},{8,7},{9,8},{10,9},{11,1... | collective-permute-start | bytes 49160 | tf_op jit(solution)/shard_map/ppermute | solution.py:213
  144.0 4.8 %collective-permute-start.7 = (f32[32,1,128]{2,1,0:T(1,128)S(1)}, f32[32,1,128]{2,1,0:T(1,128)S(1)}, u32[]{:S(2)}, u32[]{:S(2)}) collective-permute-start(f32[32,1,128]{2,1,0:T(1,128)S(1)} %get-tuple-element.29), channel_id=1, source_target_pairs={{0,1},{1,2},{2,3},{3,4},{4,5},{5,6},{6,7},{7,8},{8,9},{9,10},{10,1... | collective-permute-start | bytes 49160 | tf_op jit(solution)/shard_map/ppermute | solution.py:212
  165.7 24.6 %collective-permute-start.10 = (f32[32,1,128]{2,1,0:T(1,128)S(1)}, f32[32,1,128]{2,1,0:T(1,128)S(1)}, u32[]{:S(2)}, u32[]{:S(2)}) collective-permute-start(f32[32,1,128]{2,1,0:T(1,128)S(1)} %get-tuple-element.24), channel_id=1, source_target_pairs={{1,0},{2,1},{3,2},{4,3},{5,4},{6,5},{7,6},{8,7},{9,8},{10,9},{11,1... | collective-permute-start | bytes 49160 | tf_op jit(solution)/shard_map/ppermute | solution.py:213
  167.0 23.3 %collective-permute-start.11 = (f32[32,1,128]{2,1,0:T(1,128)S(1)}, f32[32,1,128]{2,1,0:T(1,128)S(1)}, u32[]{:S(2)}, u32[]{:S(2)}) collective-permute-start(f32[32,1,128]{2,1,0:T(1,128)S(1)} %get-tuple-element.25), channel_id=1, source_target_pairs={{0,1},{1,2},{2,3},{3,4},{4,5},{5,6},{6,7},{7,8},{8,9},{9,10},{10,1... | collective-permute-start | bytes 49160 | tf_op jit(solution)/shard_map/ppermute | solution.py:212
  171.0 19.4 %collective-permute-start.8 = (f32[1,32,128]{2,1,0:T(8,128)S(1)}, f32[1,32,128]{2,1,0:T(8,128)S(1)}, u32[]{:S(2)}, u32[]{:S(2)}) collective-permute-start(f32[1,32,128]{2,1,0:T(8,128)S(1)} %get-tuple-element.22), channel_id=1, source_target_pairs={{16,0},{32,16},{48,32},{64,48},{80,64},{96,80},{112,96},{0,112},{1... | collective-permute-start | bytes 49160 | tf_op jit(solution)/shard_map/ppermute | solution.py:213
  189.6 1.2 collective-permute-start.9

commit v2 on v1

--- a/solution.py
+++ b/solution.py
@@ -1,4 +1,4 @@
-import functools
+import itertools
 
 import jax
 import jax.numpy as jnp
@@ -202,30 +202,199 @@
 ]
 
 
-def padded(array, sides, width, wrap):
-    for axis, dim in sides:
-        devices, length = (lax.axis_size(axis), array.shape[dim])
-        up = [(i, (i + 1) % devices) for i in range(devices if wrap else devices - 1)]
-        down = [(j, i) for i, j in up]
-        last = lax.slice_in_dim(array, length - width, length, axis=dim)
-        leading = lax.slice_in_dim(array, 0, width, axis=dim)
-        before = lax.ppermute(last, axis, up)
-        after = lax.ppermute(leading, axis, down)
-        array = jnp.concatenate([before, array, after], axis=dim)
-    return array
-
-
-def smoothing(flat):
-    field = flat.reshape(CLON, CLAT, DEP)
-    lon_pad = padded(field, ((LON, 0),), 1, True)
-    lat_pad = padded(field, ((LAT, 1),), 1, False)
-    dep_pad = jnp.pad(field, ((0, 0), (0, 0), (1, 1)))
-    result = 6.0 * field - lon_pad[2:] - lon_pad[:-2] - lat_pad[:, 2:] - lat_pad[:, :-2]
-    return (result - dep_pad[:, :, 2:] - dep_pad[:, :, :-2]).reshape(COLS, DEP)
+MESH = pl.DeviceIdType.MESH
+SIZES = (4, 2, 4, 4)
+STAGES = ((1, 0), (2,), (3,))
+PEERS = max(len(list(itertools.product(*[range(SIZES[a]) for a in g]))) for g in STAGES) - 1
+
+
+def coords():
+    return tuple(lax.axis_index(a) for a in LON_LAT)
+
+
+def stage_peers(here, group):
+    found = []
+    for steps in itertools.product(*[range(SIZES[a]) for a in group]):
+        if any(steps):
+            add = dict(zip(group, steps))
+            found.append(tuple((v + add.get(i, 0)) % SIZES[i] for i, v in enumerate(here)))
+    return found
+
+
+def ring_peers(here):
+    lon, lat = here[0] * 2 + here[1], here[2] * 4 + here[3]
+    found = []
+    for step in (1, 7):
+        to = (lon + step) % 8
+        found.append((to // 2, to % 2, here[2], here[3]))
+    for step in (1, 15):
+        to = (lat + step) % 16
+        found.append((here[0], here[1], to // 4, to % 4))
+    return found
+
+
+def meet(here):
+    barrier = pltpu.get_barrier_semaphore()
+    peers = [p for g in STAGES for p in stage_peers(here, g)] + ring_peers(here)
+    for peer in peers:
+        pl.semaphore_signal(barrier, inc=1, device_id=peer, device_id_type=MESH)
+    pl.semaphore_wait(barrier, len(peers))
+
+
+def send_stage(s, here, buf, got, send_sem, recv_sem):
+    copies = []
+    for k, peer in enumerate(stage_peers(here, STAGES[s])):
+        copy = pltpu.make_async_remote_copy(
+            buf.at[s], got.at[s, k], send_sem.at[s, k], recv_sem.at[s, k], device_id=peer, device_id_type=MESH)
+        copy.start()
+        copies.append(copy)
+    return copies
+
+
+def add_stage(s, copies, buf, got):
+    total = buf[s]
+    for k, copy in enumerate(copies):
+        copy.wait_recv()
+        total = total + got[s, k]
+    return total
+
+
+def send_halo(here, field, edge, halo, send_sem, recv_sem):
+    edge[0] = field[pl.ds(CLAT - 1, CLON, stride=CLAT), :]
+    edge[1] = field[pl.ds(0, CLON, stride=CLAT), :]
+    faces = (field.at[pl.ds(COLS - CLAT, CLAT)], field.at[pl.ds(0, CLAT)], edge.at[0], edge.at[1])
+    copies = []
+    for k, (face, peer) in enumerate(zip(faces, ring_peers(here))):
+        copy = pltpu.make_async_remote_copy(
+            face, halo.at[k], send_sem.at[k], recv_sem.at[k], device_id=peer, device_id_type=MESH)
+        copy.start()
+        copies.append(copy)
+    return copies
+
+
+def stencil_rows(here, field, halo, put):
+    lat = here[2] * 4 + here[3]
+    has_before = jnp.where(lat > 0, 1.0, 0.0)
+    has_after = jnp.where(lat < 15, 1.0, 0.0)
+    row, lane = iota((CLAT, DEP), 0), iota((CLAT, DEP), 1)
+
+    def layer(i, before, after):
+        mine = pl.ds(pl.multiple_of(i * CLAT, CLAT), CLAT)
+        f = field[mine, :]
+        lat_before = jnp.where(row == 0, halo[2, pl.ds(i, 1), :] * has_before, pltpu.roll(f, 1, 0))
+        lat_after = jnp.where(row == CLAT - 1, halo[3, pl.ds(i, 1), :] * has_after, pltpu.roll(f, CLAT - 1, 0))
+        up = jnp.where(lane == 0, 0.0, pltpu.roll(f, 1, 1))
+        down = jnp.where(lane == DEP - 1, 0.0, pltpu.roll(f, DEP - 1, 1))
+        put(mine, DAMP * (6.0 * f - before - after - lat_before - lat_after - up - down))
+
+    def inner(i, carry):
+        layer(i, field[pl.ds(pl.multiple_of((i - 1) * CLAT, CLAT), CLAT), :],
+              field[pl.ds(pl.multiple_of((i + 1) * CLAT, CLAT), CLAT), :])
+        return carry
+
+    layer(0, halo[0], field[CLAT:2 * CLAT, :])
+    layer(CLON - 1, field[COLS - 2 * CLAT:COLS - CLAT, :], halo[1])
+    lax.fori_loop(1, CLON - 1, inner, 0)
+
+
+def finish(copies):
+    for copy in copies:
+        copy.wait_send()
+
+
+def middle_kernel(p_part, q, p_out, smooth, buf, got, g, edge, halo, send_sem, recv_sem, face_send, face_recv):
+    here = coords()
+    meet(here)
+    buf[0] = p_part[...]
+    first = send_stage(0, here, buf, got, send_sem, recv_sem)
+    faces = send_halo(here, q, edge.at[0], halo.at[0], face_send.at[0], face_recv.at[0])
+    buf[1] = add_stage(0, first, buf, got)
+    second = send_stage(1, here, buf, got, send_sem, recv_sem)
+    for copy in faces:
+        copy.wait_recv()
+
+    def to_g(rows, value):
+        g[rows, :] = value
+
+    stencil_rows(here, q, halo.at[0], to_g)
+    more = send_halo(here, g, edge.at[1], halo.at[1], face_send.at[1], face_recv.at[1])
+    buf[2] = add_stage(1, second, buf, got)
+    third = send_stage(2, here, buf, got, send_sem, recv_sem)
+    for copy in more:
+        copy.wait_recv()
+
+    def to_smooth(rows, value):
+        smooth[rows, :] = value
+
+    stencil_rows(here, g, halo.at[1], to_smooth)
+    p_out[...] = add_stage(2, third, buf, got)
+    finish(first + second + third + faces + more)
+
+
+def last_kernel(count, times, p_part, p0, q0, q1, model, misfit, buf, got, norm, edge, halo, send_sem, recv_sem,
+                face_send, face_recv):
+    here = coords()
+    meet(here)
+    faces = send_halo(here, q1, edge, halo, face_send, face_recv)
+    buf[0, 0:RAYS, :] = p_part[...]
+    a, b = q0[...], q1[...]
+    dots = [jnp.sum(jnp.sum(x, axis=0, keepdims=True), axis=1, keepdims=True) for x in (a * a, a * b, b * b)]
+    norm[...] = jnp.zeros_like(norm)
+    for copy in faces:
+        copy.wait_recv()
+
+    def to_norm(rows, value):
+        norm[...] += value * value
+
+    stencil_rows(here, q1, halo, to_norm)
+    dots.append(jnp.sum(jnp.sum(norm[...], axis=0, keepdims=True), axis=1, keepdims=True))
+    lane = iota((8, NDEV), 1)
+    row = jnp.zeros((8, NDEV), f32)
+    for k, dot in enumerate(dots):
+        row = jnp.where(lane == k, dot, row)
+    buf[0, RAYS:RAYS + 8, :] = row
+    sent = []
+    for s in range(len(STAGES)):
+        copies = send_stage(s, here, buf, got, send_sem, recv_sem)
+        total = add_stage(s, copies, buf, got)
+        buf[s + 1] = total
+        sent += copies
+    p1 = total[0:RAYS, :]
+    m0, m1, m2, m3 = [total[RAYS:RAYS + 1, k:k + 1] for k in range(4)]
+    m3 = m3 + jnp.sum(jnp.sum(p1 * p1, axis=0, keepdims=True), axis=1, keepdims=True)
+    r1, r2, r3 = m1 / m0, m2 / m1, m3 / m2
+    c0 = (r3 - r1) / (r3 - r2) / r1
+    c1 = (r1 - r2) / (r3 - r2) / (r1 * r2)
+    model[...] = (SCALE * c0) * a + (SCALE * c1) * b
+    me = ((here[0] * 2 + here[1]) * 4 + here[2]) * 4 + here[3]
+    fit = jnp.where(iota((RAYS, NDEV), 1) == me, c0 * p0[...] + c1 * p1, 0.0)
+    column = jnp.sum(fit, axis=1, keepdims=True)
+    own = jnp.sum(jnp.where(iota((RAYS, RAYS), 0) == iota((RAYS, RAYS), 1), column, 0.0), axis=0, keepdims=True)
+    data = jnp.where(iota((1, RAYS), 1) < count[0], times[...], 0.0)
+    misfit[...] = data - own
+    finish(faces + sent)
+
+
+def comm_scratch(rows, faces):
+    return [
+        pltpu.VMEM((len(STAGES) + 1, rows, NDEV), f32),
+        pltpu.VMEM((len(STAGES), PEERS, rows, NDEV), f32),
+    ], [
+        pltpu.VMEM(faces + (2, CLON, DEP), f32),
+        pltpu.VMEM(faces + (4, CLON, DEP), f32),
+        pltpu.SemaphoreType.DMA((len(STAGES), PEERS)),
+        pltpu.SemaphoreType.DMA((len(STAGES), PEERS)),
+        pltpu.SemaphoreType.DMA(faces + (4,)),
+        pltpu.SemaphoreType.DMA(faces + (4,)),
+    ]
+
+
+def comm_params(number):
+    return pltpu.CompilerParams(vmem_limit_bytes=16 << 20, collective_id=number, has_side_effects=True)
 
 
 def shards(travel_times, ray_counts, tile_brick, cell_offsets, cell_depths, seg_lengths):
-    live_mask = (jnp.arange(RAYS, dtype=i32) < ray_counts[0]).astype(f32)
+    times = travel_times.reshape(1, RAYS)
     send = pl.pallas_call(
         pack_kernel,
         out_shape=shape((NDEV, 5, SEG)),
@@ -233,7 +402,7 @@
         out_specs=VMEM,
         scratch_shapes=[pltpu.VMEM((128, 768), bf16)],
         compiler_params=PARAMS,
-    )(ray_counts, tile_brick, travel_times.reshape(1, RAYS), cell_offsets, cell_depths, seg_lengths)
+    )(ray_counts, tile_brick, times, cell_offsets, cell_depths, seg_lengths)
     held = lax.all_to_all(send, LON_LAT, split_axis=0, concat_axis=0, tiled=True)
     q0, p_part, col, dep, w, info, count = pl.pallas_call(
         first_kernel,
@@ -244,9 +413,15 @@
         scratch_shapes=SCRATCH,
         compiler_params=PARAMS,
     )(held)
-    p0 = lax.psum(p_part, LON_LAT)
-    g0 = DAMP * smoothing(q0)
-    smooth = DAMP * smoothing(g0)
+    bufs, faces = comm_scratch(RAYS, (2,))
+    p0, smooth = pl.pallas_call(
+        middle_kernel,
+        out_shape=(shape((RAYS, NDEV)), shape((COLS, DEP))),
+        in_specs=[VMEM] * 2,
+        out_specs=(VMEM,) * 2,
+        scratch_shapes=bufs + [pltpu.VMEM((COLS, DEP), f32)] + faces,
+        compiler_params=comm_params(0),
+    )(p_part, q0)
     q1, p_part = pl.pallas_call(
         second_kernel,
         out_shape=(shape((COLS, DEP)), shape((RAYS, NDEV))),
@@ -255,23 +430,16 @@
         scratch_shapes=SCRATCH,
         compiler_params=PARAMS,
     )(p0, smooth, col, dep, w, info, count)
-    g1 = DAMP * smoothing(q1)
-    dots = jnp.stack([jnp.sum(q0 * q0), jnp.sum(g0 * g0), jnp.sum(q1 * q1), jnp.sum(g1 * g1)])
-    row = jnp.concatenate([dots, jnp.zeros((NDEV - 4,), f32)])
-    both = lax.psum(jnp.concatenate([p_part, row[None, :]], axis=0), LON_LAT)
-    p1 = both[:RAYS]
-    m0 = both[RAYS, 0]
-    m1 = both[RAYS, 1] + jnp.sum(p0 * p0)
-    m2 = both[RAYS, 2]
-    m3 = both[RAYS, 3] + jnp.sum(p1 * p1)
-    r1, r2, r3 = m1 / m0, m2 / m1, m3 / m2
-    c0 = (r3 - r1) / (r3 - r2) / r1
-    c1 = (r1 - r2) / (r3 - r2) / (r1 * r2)
-    model = SCALE * (c0 * q0 + c1 * q1)
-    me = lax.axis_index(LON_LAT)
-    mine = lambda p: lax.dynamic_slice_in_dim(p, me, 1, axis=1)[:, 0]
-    misfit = travel_times * live_mask - c0 * mine(p0) - c1 * mine(p1)
-    return (model.reshape(CLON, CLAT, DEP), misfit)
+    bufs, faces = comm_scratch(RAYS + 8, ())
+    model, misfit = pl.pallas_call(
+        last_kernel,
+        out_shape=(shape((COLS, DEP)), shape((1, RAYS))),
+        in_specs=[SMEM] + [VMEM] * 5,
+        out_specs=(VMEM,) * 2,
+        scratch_shapes=bufs + [pltpu.VMEM((CLAT, DEP), f32)] + faces,
+        compiler_params=comm_params(1),
+    )(ray_counts, times, p_part, p0, q0, q1)
+    return (model.reshape(CLON, CLAT, DEP), misfit.reshape(RAYS))
 
 
 def solution(mesh):

time: 273 us -> 136 us (0.50)
  blocking collectives: 135 us -> 24.6 us
  Pallas kernels: 36 us -> 104 us
  starting transfers between devices: 66.1 us -> 0 us
  waiting for transfers between devices: 14 us -> 0 us
  other arithmetic: 6.79 us -> 0 us
  between operations: 6.66 us -> 1.32 us
    psum x2 -> x0, blocking collectives: 135 us -> none  [the longest x1 69.6 us: shards(): both = lax.psum(jnp.concatenate([p_part, row[None, :]], axis=0), LON_LAT)]
    pallas_call x0 -> x2, Pallas kernels: none -> 75.2 us  [the longest x1 41.2 us: shards(): pl.pallas_call(last_kernel, out_shape=(shape((COLS, DEP)), shape((1, RAYS...]
    ppermute x12 -> x0, starting transfers between devices: 54.6 us -> none  [the longest x6 40.7 us: padded(): after = lax.ppermute(leading, axis, down)]
    all_to_all x0 -> x1, blocking collectives: none -> 24.6 us  [shards(): lax.all_to_all(send, LON_LAT, split_axis=0, concat_axis=0, tiled=True)]
    all_to_all x1 -> x0, waiting for transfers between devices: 13.3 us -> none  [shards(): lax.all_to_all(send, LON_LAT, split_axis=0, concat_axis=0, tiled=True)]
    all_to_all x1 -> x0, starting transfers between devices: 11.5 us -> none  [shards(): lax.all_to_all(send, LON_LAT, split_axis=0, concat_axis=0, tiled=True)]
    reduce_sum x5 -> x0, other arithmetic: 4.17 us -> none  [the longest x1 1.01 us: shards(): jnp.sum(g1 * g1)]
    pallas_call x1, Pallas kernels: 16.5 us -> 13.1 us  [shards(): pl.pallas_call(second_kernel, out_shape=(shape((COLS, DEP)), shape((RAYS,...]
  transfers between devices with their start and end apart: 13 -> 0, of which waited for: 4 -> 0; matrix products, arithmetic and copies ran while one was open for 1% -> 0% of each run, Pallas kernels for 0% -> 0%
where the time goes in v2:
time: 136 us; the launch traced here: 135 us
  Pallas kernels  104 us (76%)
  blocking collectives  24.6 us (18%)
  local copies, waits for them, and re-layouts  5.24 us (4%)
    pallas_call x1, Pallas kernels, shards(): pl.pallas_call(last_kernel, out_shape=(shape((COLS, DEP)), shape((1, RAYS...  41.2 us
    pallas_call x1, Pallas kernels, shards(): pl.pallas_call(middle_kernel, out_shape=(shape((RAYS, NDEV)), shape((COLS...  34.1 us
    all_to_all x1, blocking collectives, shards(): lax.all_to_all(send, LON_LAT, split_axis=0, concat_axis=0, tiled=True)  24.6 us
    pallas_call x1, Pallas kernels, shards(): pl.pallas_call(first_kernel, out_shape=(shape((COLS, DEP)), shape((RAYS,...  14.3 us
    pallas_call x1, Pallas kernels, shards(): pl.pallas_call(second_kernel, out_shape=(shape((COLS, DEP)), shape((RAYS,...  13.1 us
    unnamed x11, local copies, waits for them, and re-layouts  5.24 us

profile of v2, /device:TPU:1, one launch (start us, length us, event | category | flops | bytes accessed | tf_op | source)
XLA Modules:
  0.0 134.8 jit_solution(2396733909273404698)
XLA Ops:
  1.3 0.8 copy.8.brick
  2.0 0.0 copy-start.3
  2.0 0.7 copy-done.3
  2.7 0.0 copy-start
  2.7 0.8 copy-done
  3.5 0.0 copy-start.1
  3.5 0.8 copy-done.1
  4.4 0.0 copy-start.2
  4.4 0.8 copy-done.2
  5.2 1.1 shard_map.77
  6.3 24.6 %all_to_all.5.held = f32[128,5,128]{2,1,0:T(8,128)S(1)} all-to-all(f32[128,5,128]{2,1,0:T(8,128)S(1)} %shard_map.77), channel_id=1, replica_groups=mesh['lon_0'=4,'lon_1'=2,'lat_0'=4,'lat_1'=4] {'lon_0','lon_1','lat_0','..., dimensions={0} | all-to-all | bytes 655360 | tf_op jit(solution)/shard_map/all_to_all | solution.py:406
  31.0 14.3 %shard_map.78 = (f32[1024,128]{1,0:T(8,128)S(1)}, f32[32,128]{1,0:T(8,128)S(1)}, s32[256,128]{1,0:T(8,128)S(1)}, s32[256,128]{1,0:T(8,128)S(1)}, f32[256,128]{1,...) custom-call(f32[128,5,128]{2,1,0:T(8,128)S(1)} %all_to_all.5.held), custom_call_target="tpu_custom_call" | custom-call | tf_op jit(solution)/shard_map/pallas_call | solution.py:407
  45.2 34.1 %shard_map.79 = (f32[32,128]{1,0:T(8,128)S(1)}, f32[1024,128]{1,0:T(8,128)S(1)}) custom-call(f32[32,128]{1,0:T(8,128)S(1)} %get-tuple-element.15.p_part, f32[1024,128]{1,0:T(8,128)S(1)} %get-tuple-element.16.q.q0), custom_call_target="tpu_custom_call" | custom-call | tf_op jit(solution)/shard_map/pallas_call | solution.py:417
  79.3 13.1 %shard_map.80 = (f32[1024,128]{1,0:T(8,128)S(1)}, f32[32,128]{1,0:T(8,128)S(1)}) custom-call(f32[32,128]{1,0:T(8,128)S(1)} %get-tuple-element.17.p.p0, f32[1024,128]{1,0:T(8,128)S(1)} %get-tuple-element.18.smooth, s32[256,128]{1,0:T(8,128)S(1)} %get-tuple-element.19.col, s32[256,128]{1,0:T(8,128)S(1)} %get-tuple-element.20.dep, ...), custom_call_target="tpu_custom_call" | custom-call | tf_op jit(solution)/shard_map/pallas_call | solution.py:425
  92.4 41.2 %shard_map.81 = (f32[1024,128]{1,0:T(8,128)S(1)}, f32[1,32]{1,0:T(1,128)S(1)}) custom-call(s32[1]{0:T(128)S(6)} %copy.11.count, f32[1,32]{1,0:T(1,128)S(1)} %bitcast.5, f32[32,128]{1,0:T(8,128)S(1)} %get-tuple-element.24.p_part, f32[32,128]{1,0:T(8,128)S(1)} %get-tuple-element.17.p.p0, f32[1024,128]{1,0:T(8,128)S(1)} %get-tuple-element.16.q.q0, ...), custom_call_target="tpu_custom_call" | custom-call | tf_op jit(solution)/shard_map/pallas_call | solution.py:434
  133.5 0.8 copy.12
  134.3 0.5 copy.13
Async XLA Ops:
  2.0 0.7 copy-start.3
  2.7 0.8 copy-start
  3.5 0.8 copy-start.1
  4.4 0.8 copy-start.2

commit v3 on v2

--- a/solution.py
+++ b/solution.py
@@ -14,13 +14,14 @@
 NDEV = 128
 SLOTS = 2 * NDEV
 CHUNK = 8
+BLOCKS, BLOCK, HALF = 4, 256, 64
 SCALE = 8.0
 DAMP = 0.01 * SCALE
 LON_LAT = ("lon_0", "lon_1", "lat_0", "lat_1")
 LON = ("lon_0", "lon_1")
 LAT = ("lat_0", "lat_1")
 
-f32, bf16, i32 = jnp.float32, jnp.bfloat16, jnp.int32
+f32, bf16, i32, i16 = jnp.float32, jnp.bfloat16, jnp.int32, jnp.int16
 VMEM = pl.BlockSpec(memory_space=pltpu.VMEM)
 SMEM = pl.BlockSpec(memory_space=pltpu.SMEM)
 PARAMS = pltpu.CompilerParams(vmem_limit_bytes=48 << 20)
@@ -53,20 +54,23 @@
     return z, high * 128.0 + low, (hi + mid) + lo
 
 
-def pack_kernel(count, brick, times, offs, deps, lens, out, pay):
-    lane = iota((RAYS, 128), 1)
-    mine = iota((RAYS, 128), 0) == (lane & 31)
-    tb = brick[...]
-    wide = jnp.zeros((RAYS, 128), i32)
-    for k in range(TPR):
-        wide = jnp.where((lane >> 5) == k, tb[:, k:k + 1], wide)
-    brick_row = jnp.sum(jnp.where(mine, wide, 0).astype(f32), axis=0, keepdims=True)
+def pack_kernel(count, brick, times, offs_in, deps_in, lens_in, out, pay, offs, deps, lens, sem):
+    loads = [
+        pltpu.make_async_copy(src, dst, sem.at[k])
+        for k, (src, dst) in enumerate(((offs_in, offs), (deps_in, deps), (lens_in, lens)))
+    ]
+    for load in loads:
+        load.start()
+    tb = brick[...].astype(f32)
+    brick_row = jnp.concatenate([tb[k:k + 1, :] for k in range(TPR)], axis=1)
     time_row = jnp.concatenate([times[...]] * TPR, axis=1)
     ray_row = iota((1, 128), 1) & 31
     live = ray_row < count[0]
     as_rows = jnp.broadcast_to(brick_row, (128, 128))
     same = (as_rows == as_rows.T) & (iota((128, 128), 0) < iota((128, 128), 1))
     rank_row = jnp.sum(jnp.where(same, 1.0, 0.0), axis=0, keepdims=True)
+    for load in loads:
+        load.wait()
     for k in range(TPR):
         cell = offs[:, k, :] * DEP + deps[:, k, :]
         pay[k * RAYS:(k + 1) * RAYS, :] = as_payload(cell, lens[:, k, :] * SCALE)
@@ -85,48 +89,119 @@
 
 
 def onehot_cols(col_row):
-    at = jnp.broadcast_to(col_row.astype(jnp.int16), (COLS, 128))
-    return jnp.where(lax.broadcasted_iota(jnp.int16, (COLS, 128), 0) == at, jnp.ones((), bf16), jnp.zeros((), bf16))
-
-
-def scatter_into(acc, n, col, dep, wy, oht, vt):
+    at = jnp.broadcast_to(col_row.astype(i16), (BLOCK, 128))
+    return jnp.where(lax.broadcasted_iota(i16, (BLOCK, 128), 0) == at, jnp.ones((), bf16), jnp.zeros((), bf16))
+
+
+def onehot_values(dep_row, val_row):
+    at = jnp.broadcast_to(dep_row.astype(i16), (DEP, 128))
+    here = lax.broadcasted_iota(i16, (DEP, 128), 0) == at
+    return jnp.concatenate(
+        [jnp.where(here, jnp.broadcast_to(part, (DEP, 128)), jnp.zeros((), bf16)) for part in split2(val_row)], axis=0)
+
+
+def scatter_rows(acc, chunks, col, dep, val):
     acc[...] = jnp.zeros_like(acc)
 
     def body(c, carry):
-        for j in range(CHUNK):
-            row = pl.ds(c * CHUNK + j, 1)
-            at = slice(j * 128, (j + 1) * 128)
-            oht[:, at] = onehot_cols(col[row, :])
-            w = wy[row, :]
-            hi = w.astype(bf16).astype(f32)
-            here = iota((DEP, 128), 0) == dep[row, :]
-            vt[0:128, at] = jnp.where(here, hi, 0.0).astype(bf16)
-            vt[128:256, at] = jnp.where(here, w - hi, 0.0).astype(bf16)
-        acc[...] += lax.dot_general(oht[...], vt[...], (((1,), (1,)), ((), ())), preferred_element_type=f32)
+        rows = [pl.ds(c * CHUNK + j, 1) for j in range(CHUNK)]
+        for b in range(BLOCKS):
+            left = jnp.concatenate([onehot_cols(col(b, r)) for r in rows], axis=1)
+            right = jnp.concatenate([onehot_values(dep(b, r), val(b, r)) for r in rows], axis=1)
+            acc[b] += lax.dot_general(left, right, (((1,), (1,)), ((), ())), preferred_element_type=f32)
         return carry
 
-    lax.fori_loop(0, (n + CHUNK - 1) // CHUNK, body, 0)
-
-
-def gather_from(grid, n, col, dep, w, out, oht, gt):
-    hi, lo = split2(grid.T)
-    gt[0:128, :] = hi
-    gt[128:256, :] = lo
+    lax.fori_loop(0, chunks, body, 0)
+
+
+def gather_rows(gt, chunks, col, dep, w, out):
     out[...] = jnp.zeros_like(out)
 
     def body(c, carry):
-        for j in range(CHUNK):
-            oht[:, j * 128:(j + 1) * 128] = onehot_cols(col[pl.ds(c * CHUNK + j, 1), :])
-        res = jnp.dot(gt[...], oht[...], preferred_element_type=f32)
-        for j in range(CHUNK):
-            row = pl.ds(c * CHUNK + j, 1)
-            at = slice(j * 128, (j + 1) * 128)
-            both = res[0:128, at] + res[128:256, at]
-            here = iota((DEP, 128), 0) == dep[row, :]
-            out[row, :] = jnp.sum(jnp.where(here, both, 0.0), axis=0, keepdims=True) * w[row, :]
+        rows = [pl.ds(c * CHUNK + j, 1) for j in range(CHUNK)]
+        sums = [jnp.zeros((8, 128), f32)] * CHUNK
+        for b in range(BLOCKS):
+            right = jnp.concatenate([onehot_cols(col(b, r)) for r in rows], axis=1)
+            res = jnp.dot(gt[:, b * BLOCK:(b + 1) * BLOCK], right, preferred_element_type=f32)
+            for j, r in enumerate(rows):
+                at = slice(j * 128, (j + 1) * 128)
+                both = res[0:128, at] + res[128:256, at]
+                here = jnp.where(iota((DEP, 128), 0) == dep(b, r), both, 0.0)
+                sums[j] = sums[j] + here.reshape(16, 8, 128).sum(axis=0) * w(b, r)
+        for j, r in enumerate(rows):
+            out[r, :] = jnp.sum(sums[j], axis=0, keepdims=True)
         return carry
 
-    lax.fori_loop(0, (n + CHUNK - 1) // CHUNK, body, 0)
+    lax.fori_loop(0, chunks, body, 0)
+
+
+def pair(x):
+    x = x.reshape(16, 16, 128)
+    return jnp.where(iota((16, 8, 128), 2) < HALF, x[:, 0:8], x[:, 8:16]).reshape(128, 128)
+
+
+def unpair(x):
+    low = iota((128, 128), 1) < HALF
+    halves = [jnp.sum(jnp.where(m, x, 0.0), axis=1, keepdims=True) for m in (low, ~low)]
+    return jnp.concatenate([h.reshape(16, 8, 1) for h in halves], axis=1).reshape(SLOTS, 1)
+
+
+def take(x, index):
+    return jnp.take_along_axis(x, index, axis=1, mode="promise_in_bounds")
+
+
+def bucket(n, col, dep, w, bcol, bdep, bw):
+    upto = jnp.where(iota((128, 128), 0) <= iota((128, 128), 1), 1.0, 0.0).astype(bf16)
+    rank = iota((SLOTS, 128), 1) & (HALF - 1)
+    most = jnp.zeros((SLOTS, 1), i32)
+    for b in range(BLOCKS):
+        inside = jnp.where((col >> 8) == b, 1.0, 0.0).astype(bf16)
+        counts = jnp.dot(inside, upto, preferred_element_type=f32).astype(i32)
+        at = jnp.zeros((SLOTS, 128), i32)
+        for step in (64, 32, 16, 8, 4, 2, 1):
+            at = jnp.where(take(counts, at + (step - 1)) <= rank, at + step, at)
+        held = counts[:, 127:128]
+        bcol[b] = pair(take(col, at) - b * BLOCK)
+        bdep[b] = pair(take(dep, at))
+        bw[b] = pair(jnp.where(rank < held, take(w, at), 0.0))
+        most = jnp.maximum(most, held)
+    most = jnp.where(iota((SLOTS, 1), 0) < n, most, 0)
+    return jnp.max(most.astype(f32)).astype(i32)
+
+
+def both_passes(n, most, y_col, col, dep, w, bcol, bdep, bw, extra, q_out, acc, gt, wy, vals, part):
+    fits = most <= HALF
+
+    def whole():
+        q = jnp.concatenate([acc[b, :, 0:128] + acc[b, :, 128:256] for b in range(BLOCKS)], axis=0)
+        if extra is not None:
+            q = q + extra[...]
+        q_out[...] = q
+        hi, lo = split2(q.T)
+        gt[0:128, :] = hi
+        gt[128:256, :] = lo
+
+    @pl.when(fits)
+    def _():
+        chunks = (n + 2 * CHUNK - 1) // (2 * CHUNK)
+        y = pair(jnp.broadcast_to(y_col, (SLOTS, 128)))
+        for b in range(BLOCKS):
+            wy[b] = bw[b] * y
+        cols, deps = (lambda b, r: bcol[b, r, :]), (lambda b, r: bdep[b, r, :])
+        scatter_rows(acc, chunks, cols, deps, lambda b, r: wy[b, r, :])
+        whole()
+        gather_rows(gt, chunks, cols, deps, lambda b, r: bw[b, r, :], vals.at[pl.ds(0, 128)])
+        part[...] = unpair(vals[0:128, :])
+
+    @pl.when(jnp.logical_not(fits))
+    def _():
+        chunks = (n + CHUNK - 1) // CHUNK
+        vals[...] = w[...] * y_col
+        cols, deps = (lambda b, r: col[r, :] - b * BLOCK), (lambda b, r: dep[r, :])
+        scatter_rows(acc, chunks, cols, deps, lambda b, r: vals[r, :])
+        whole()
+        gather_rows(gt, chunks, cols, deps, lambda b, r: w[r, :], vals)
+        part[...] = jnp.sum(vals[...], axis=1, keepdims=True)
 
 
 def place_of(slot_info):
@@ -150,7 +225,7 @@
     return jnp.sum(place * jnp.concatenate(rows, axis=1), axis=1, keepdims=True)
 
 
-def first_kernel(held, q_out, p_out, col, dep, w, info, count, oht, vt, acc, gt, wy):
+def first_kernel(held, q_out, p_out, col, dep, w, bcol, bdep, bw, info, count, acc, gt, wy, vals, part):
     meta = held[:, 4, :].T
     y_row = jnp.concatenate([meta[0:1, :], meta[1:2, :]], axis=1)
     ray_row = jnp.concatenate([meta[2:3, :], meta[3:4, :]], axis=1).astype(i32) - 1
@@ -162,31 +237,26 @@
     info[0:1, :] = at
     info[1:2, :] = ray_row
     n = jnp.sum(jnp.where(live, 1.0, 0.0)).astype(i32)
-    count[0] = n
     place = place_of(at)
     pay = jnp.concatenate([as_payload(held[:, k, :].astype(i32), held[:, 2 + k, :]) for k in range(2)], axis=0)
     z, c, lens = from_payload(jnp.dot(place.astype(bf16), pay, preferred_element_type=f32))
     col[...] = c.astype(i32)
     dep[...] = z.astype(i32)
     w[...] = lens
-    wy[...] = lens * jnp.sum(place * y_row, axis=1, keepdims=True)
-    scatter_into(acc, n, col, dep, wy, oht, vt)
-    q = acc[:, 0:128] + acc[:, 128:256]
-    q_out[...] = q
-    gather_from(q, n, col, dep, w, wy, oht, gt)
-    p_out[...] = to_rays(jnp.sum(wy[...], axis=1, keepdims=True), place, ray_row)
-
-
-def second_kernel(p, smooth, col, dep, w, info, count, q_out, p_out, oht, vt, acc, gt, wy):
-    n = count[0]
+    most = bucket(n, col[...], dep[...], lens, bcol, bdep, bw)
+    count[0] = n
+    count[1] = most
+    y_col = jnp.sum(place * y_row, axis=1, keepdims=True)
+    both_passes(n, most, y_col, col, dep, w, bcol, bdep, bw, None, q_out, acc, gt, wy, vals, part)
+    p_out[...] = to_rays(part[...], place_of(at), ray_row)
+
+
+def second_kernel(p, smooth, col, dep, w, bcol, bdep, bw, info, count, q_out, p_out, acc, gt, wy, vals, part):
     place = place_of(info[0:1, :])
     ray_row = info[1:2, :]
-    wy[...] = w[...] * from_rays(p[...], place, ray_row)
-    scatter_into(acc, n, col, dep, wy, oht, vt)
-    q = acc[:, 0:128] + acc[:, 128:256] + smooth[...]
-    q_out[...] = q
-    gather_from(q, n, col, dep, w, wy, oht, gt)
-    p_out[...] = to_rays(jnp.sum(wy[...], axis=1, keepdims=True), place, ray_row)
+    y_col = from_rays(p[...], place, ray_row)
+    both_passes(count[0], count[1], y_col, col, dep, w, bcol, bdep, bw, smooth, q_out, acc, gt, wy, vals, part)
+    p_out[...] = to_rays(part[...], place, ray_row)
 
 
 def shape(dims, dtype=f32):
@@ -194,11 +264,11 @@
 
 
 SCRATCH = [
-    pltpu.VMEM((COLS, CHUNK * 128), bf16),
-    pltpu.VMEM((256, CHUNK * 128), bf16),
-    pltpu.VMEM((COLS, 256), f32),
+    pltpu.VMEM((BLOCKS, BLOCK, 256), f32),
     pltpu.VMEM((256, COLS), bf16),
+    pltpu.VMEM((BLOCKS, 128, 128), f32),
     pltpu.VMEM((SLOTS, SEG), f32),
+    pltpu.VMEM((SLOTS, 1), f32),
 ]
 
 
@@ -398,18 +468,19 @@
     send = pl.pallas_call(
         pack_kernel,
         out_shape=shape((NDEV, 5, SEG)),
-        in_specs=[SMEM] + [VMEM] * 5,
+        in_specs=[SMEM] + [VMEM] * 2 + [pl.BlockSpec(memory_space=pl.ANY)] * 3,
         out_specs=VMEM,
-        scratch_shapes=[pltpu.VMEM((128, 768), bf16)],
+        scratch_shapes=[pltpu.VMEM((128, 768), bf16)] + [pltpu.VMEM((RAYS, TPR, SEG), d) for d in (i32, i32, f32)]
+        + [pltpu.SemaphoreType.DMA((3,))],
         compiler_params=PARAMS,
-    )(ray_counts, tile_brick, times, cell_offsets, cell_depths, seg_lengths)
+    )(ray_counts, tile_brick.T, times, cell_offsets, cell_depths, seg_lengths)
     held = lax.all_to_all(send, LON_LAT, split_axis=0, concat_axis=0, tiled=True)
-    q0, p_part, col, dep, w, info, count = pl.pallas_call(
+    entries = [shape((SLOTS, SEG), d) for d in (i32, i32, f32)] + [shape((BLOCKS, 128, 128), d) for d in (i32, i32, f32)]
+    q0, p_part, *lists, info, count = pl.pallas_call(
         first_kernel,
-        out_shape=(shape((COLS, DEP)), shape((RAYS, NDEV)), shape((SLOTS, SEG), i32), shape((SLOTS, SEG), i32),
-                   shape((SLOTS, SEG)), shape((2, SLOTS), i32), shape((1,), i32)),
+        out_shape=(shape((COLS, DEP)), shape((RAYS, NDEV)), *entries, shape((2, SLOTS), i32), shape((2,), i32)),
         in_specs=[VMEM],
-        out_specs=(VMEM,) * 6 + (SMEM,),
+        out_specs=(VMEM,) * 9 + (SMEM,),
         scratch_shapes=SCRATCH,
         compiler_params=PARAMS,
     )(held)
@@ -425,11 +496,11 @@
     q1, p_part = pl.pallas_call(
         second_kernel,
         out_shape=(shape((COLS, DEP)), shape((RAYS, NDEV))),
-        in_specs=[VMEM] * 6 + [SMEM],
+        in_specs=[VMEM] * 9 + [SMEM],
         out_specs=(VMEM,) * 2,
         scratch_shapes=SCRATCH,
         compiler_params=PARAMS,
-    )(p0, smooth, col, dep, w, info, count)
+    )(p0, smooth, *lists, info, count)
     bufs, faces = comm_scratch(RAYS + 8, ())
     model, misfit = pl.pallas_call(
         last_kernel,

time: 136 us -> 104 us (0.76)
  Pallas kernels: 104 us -> 72.6 us
    pallas_call x1, Pallas kernels: 41.2 us -> 28.4 us  [shards(): pl.pallas_call(last_kernel, out_shape=(shape((COLS, DEP)), shape((1, RAYS...]
    pallas_call x1, Pallas kernels: 34.1 us -> 23.3 us  [shards(): pl.pallas_call(middle_kernel, out_shape=(shape((RAYS, NDEV)), shape((COLS...]
    pallas_call x1, Pallas kernels: 13.1 us -> 7.26 us  [shards(): pl.pallas_call(second_kernel, out_shape=(shape((COLS, DEP)), shape((RAYS,...]
    pallas_call x1, Pallas kernels: 14.3 us -> 12.3 us  [shards(): pl.pallas_call(first_kernel, out_shape=(shape((COLS, DEP)), shape((RAYS,...]
    unnamed x11 -> x12, local copies, waits for them, and re-layouts: 5.24 us -> 4.49 us
where the time goes in v3:
time: 104 us; the launch traced here: 103 us
  Pallas kernels  72.6 us (70%)
  blocking collectives  24.6 us (24%)
  local copies, waits for them, and re-layouts  4.49 us (4%)
  between operations  1.33 us (1%)
    pallas_call x1, Pallas kernels, shards(): pl.pallas_call(last_kernel, out_shape=(shape((COLS, DEP)), shape((1, RAYS...  28.4 us
    all_to_all x1, blocking collectives, shards(): lax.all_to_all(send, LON_LAT, split_axis=0, concat_axis=0, tiled=True)  24.6 us
    pallas_call x1, Pallas kernels, shards(): pl.pallas_call(middle_kernel, out_shape=(shape((RAYS, NDEV)), shape((COLS...  23.3 us
    pallas_call x1, Pallas kernels, shards(): pl.pallas_call(first_kernel, out_shape=(shape((COLS, DEP)), shape((RAYS,...  12.3 us
    pallas_call x1, Pallas kernels, shards(): pl.pallas_call(second_kernel, out_shape=(shape((COLS, DEP)), shape((RAYS,...  7.26 us
    unnamed x12, local copies, waits for them, and re-layouts  4.49 us

profile of v3, /device:TPU:1, one launch (start us, length us, event | category | flops | bytes accessed | tf_op | source)
XLA Modules:
  0.0 103.0 jit_solution(13056174921718956486)
XLA Ops:
  1.3 0.0 copy-start.4
  1.3 0.0 copy-start.3
  1.3 0.7 copy-done.4
  2.0 0.0 copy-done.3
  2.0 0.0 copy-start
  2.0 0.8 copy-done
  2.8 0.0 copy-start.1
  2.8 0.8 copy-done.1
  3.6 0.0 copy-start.2
  3.6 0.8 copy-done.2
  4.5 1.4 %shard_map.77 = f32[128,5,128]{2,1,0:T(8,128)S(1)} custom-call(s32[1]{0:T(128)S(6)} %copy.10.count, s32[4,32]{1,0:T(4,128)S(1)} %bitcast.7, f32[1,32]{1,0:T(1,128)S(1)} %bitcast.5, s32[32,4,128]{2,1,0:T(4,128)S(1)} %copy-done, s32[32,4,128]{2,1,0:T(4,128)S(1)} %copy-done.1, f32[32,4,128]{2,1,0:T(4,128)S(1)} %copy-done.2), custom_call_target="tpu_custom_call" | custom-call | tf_op jit(solution)/shard_map/pallas_call | solution.py:468
  5.9 24.6 %all_to_all.5.held = f32[128,5,128]{2,1,0:T(8,128)S(1)} all-to-all(f32[128,5,128]{2,1,0:T(8,128)S(1)} %shard_map.77), channel_id=1, replica_groups=mesh['lon_0'=4,'lon_1'=2,'lat_0'=4,'lat_1'=4] {'lon_0','lon_1','lat_0','..., dimensions={0} | all-to-all | bytes 655360 | tf_op jit(solution)/shard_map/all_to_all | solution.py:477
  30.5 12.3 %shard_map.78 = (f32[1024,128]{1,0:T(8,128)S(1)}, f32[32,128]{1,0:T(8,128)S(1)}, s32[256,128]{1,0:T(8,128)S(1)}, s32[256,128]{1,0:T(8,128)S(1)}, f32[256,128]{1,...) custom-call(f32[128,5,128]{2,1,0:T(8,128)S(1)} %all_to_all.5.held), custom_call_target="tpu_custom_call" | custom-call | tf_op jit(solution)/shard_map/pallas_call | solution.py:479
  42.8 23.3 %shard_map.79 = (f32[32,128]{1,0:T(8,128)S(1)}, f32[1024,128]{1,0:T(8,128)S(1)}) custom-call(f32[32,128]{1,0:T(8,128)S(1)} %get-tuple-element.18.p_part, f32[1024,128]{1,0:T(8,128)S(1)} %get-tuple-element.19.q.q0), custom_call_target="tpu_custom_call" | custom-call | tf_op jit(solution)/shard_map/pallas_call | solution.py:488
  66.1 7.3 %shard_map.80 = (f32[1024,128]{1,0:T(8,128)S(1)}, f32[32,128]{1,0:T(8,128)S(1)}) custom-call(f32[32,128]{1,0:T(8,128)S(1)} %get-tuple-element.20.p.p0, f32[1024,128]{1,0:T(8,128)S(1)} %get-tuple-element.21.smooth, s32[256,128]{1,0:T(8,128)S(1)} %get-tuple-element.22.col, s32[256,128]{1,0:T(8,128)S(1)} %get-tuple-element.23.dep, ...), custom_call_target="tpu_custom_call" | custom-call | tf_op jit(solution)/shard_map/pallas_call | solution.py:496
  73.4 28.4 %shard_map.81 = (f32[1024,128]{1,0:T(8,128)S(1)}, f32[1,32]{1,0:T(1,128)S(1)}) custom-call(s32[1]{0:T(128)S(6)} %copy.10.count, f32[1,32]{1,0:T(1,128)S(1)} %bitcast.6, f32[32,128]{1,0:T(8,128)S(1)} %get-tuple-element.30.p_part, f32[32,128]{1,0:T(8,128)S(1)} %get-tuple-element.20.p.p0, f32[1024,128]{1,0:T(8,128)S(1)} %get-tuple-element.19.q.q0, ...), custom_call_target="tpu_custom_call" | custom-call | tf_op jit(solution)/shard_map/pallas_call | solution.py:505
  101.7 0.8 copy.11
  102.5 0.5 copy.12
Async XLA Ops:
  1.3 0.7 copy-start.4
  1.3 0.7 copy-start.3
  2.0 0.8 copy-start
  2.8 0.8 copy-start.1
  3.6 0.8 copy-start.2

commit v4 on v3

--- a/solution.py
+++ b/solution.py
@@ -27,6 +27,46 @@
 PARAMS = pltpu.CompilerParams(vmem_limit_bytes=48 << 20)
 
 
+MESH = pl.DeviceIdType.MESH
+SIZES = (4, 2, 4, 4)
+
+
+def coords():
+    return tuple(lax.axis_index(a) for a in LON_LAT)
+
+
+def flat(at):
+    return ((at[0] * 2 + at[1]) * 4 + at[2]) * 4 + at[3]
+
+
+def stage_peers(here, group):
+    found = []
+    for steps in itertools.product(*[range(SIZES[a]) for a in group]):
+        if any(steps):
+            add = dict(zip(group, steps))
+            found.append(tuple((v + add.get(i, 0)) % SIZES[i] for i, v in enumerate(here)))
+    return found
+
+
+def ring_peers(here):
+    lon, lat = here[0] * 2 + here[1], here[2] * 4 + here[3]
+    found = []
+    for step in (1, 7):
+        to = (lon + step) % 8
+        found.append((to // 2, to % 2, here[2], here[3]))
+    for step in (1, 15):
+        to = (lat + step) % 16
+        found.append((here[0], here[1], to // 4, to % 4))
+    return found
+
+
+def meet(peers):
+    barrier = pltpu.get_barrier_semaphore()
+    for peer in peers:
+        pl.semaphore_signal(barrier, inc=1, device_id=peer, device_id_type=MESH)
+    pl.semaphore_wait(barrier, len(peers))
+
+
 def iota(shape, dim):
     return lax.broadcasted_iota(i32, shape, dim)
 
@@ -54,13 +94,51 @@
     return z, high * 128.0 + low, (hi + mid) + lo
 
 
-def pack_kernel(count, brick, times, offs_in, deps_in, lens_in, out, pay, offs, deps, lens, sem):
+def prefix(flags):
+    upto = jnp.where(iota((128, 128), 0) <= iota((128, 128), 1), 1.0, 0.0).astype(bf16)
+    return jnp.dot(jnp.where(flags, 1.0, 0.0).astype(bf16), upto, preferred_element_type=f32).astype(i32)
+
+
+def take(x, index):
+    return jnp.take_along_axis(x, index, axis=1, mode="promise_in_bounds")
+
+
+def by_block(cell, w):
+    counts = [prefix((cell >> 15) == b) for b in range(BLOCKS)]
+    starts = [jnp.zeros((128, 1), i32)]
+    for b in range(BLOCKS - 1):
+        starts.append(starts[-1] + counts[b][:, 127:128])
+    lane = iota((128, 128), 1)
+    block, rank = jnp.zeros((128, 128), i32), lane
+    for b in range(1, BLOCKS):
+        block = jnp.where(lane >= starts[b], b, block)
+        rank = jnp.where(lane >= starts[b], lane - starts[b], rank)
+    at = jnp.zeros((128, 128), i32)
+    for step in (64, 32, 16, 8, 4, 2, 1):
+        probe = at + (step - 1)
+        seen = take(counts[0], probe)
+        for b in range(1, BLOCKS):
+            seen = jnp.where(block == b, take(counts[b], probe), seen)
+        at = jnp.where(seen <= rank, at + step, at)
+    marks = jnp.zeros((128, 128), f32)
+    for b in range(1, BLOCKS):
+        marks = jnp.where((lane == 4 + b) | (lane == 8 + b), starts[b].astype(f32), marks)
+    return take(cell, at), take(w, at), marks
+
+
+def send_kernel(count, brick, times, offs_in, deps_in, lens_in, held, send, pay, offs, deps, lens, load_sem, meet_sem,
+                send_sem, recv_sem):
+    here = coords()
     loads = [
-        pltpu.make_async_copy(src, dst, sem.at[k])
+        pltpu.make_async_copy(src, dst, load_sem.at[k])
         for k, (src, dst) in enumerate(((offs_in, offs), (deps_in, deps), (lens_in, lens)))
     ]
     for load in loads:
         load.start()
+    barrier = pltpu.get_barrier_semaphore()
+    lines = [p for axis in range(4) for p in stage_peers(here, (axis,))]
+    for peer in lines:
+        pl.semaphore_signal(barrier, inc=1, device_id=peer, device_id_type=MESH)
     tb = brick[...].astype(f32)
     brick_row = jnp.concatenate([tb[k:k + 1, :] for k in range(TPR)], axis=1)
     time_row = jnp.concatenate([times[...]] * TPR, axis=1)
@@ -71,21 +149,51 @@
     rank_row = jnp.sum(jnp.where(same, 1.0, 0.0), axis=0, keepdims=True)
     for load in loads:
         load.wait()
-    for k in range(TPR):
-        cell = offs[:, k, :] * DEP + deps[:, k, :]
-        pay[k * RAYS:(k + 1) * RAYS, :] = as_payload(cell, lens[:, k, :] * SCALE)
-    target = iota((128, 128), 0).astype(f32)
-    meta = jnp.zeros((128, 128), f32)
+    cell = jnp.concatenate([offs[:, k, :] * DEP + deps[:, k, :] for k in range(TPR)], axis=0)
+    w = jnp.concatenate([lens[:, k, :] * SCALE for k in range(TPR)], axis=0)
+    cell, w, marks = by_block(cell, w)
+    pay[:, 0:768] = as_payload(cell, w)
+    pay[:, 768:896] = marks.astype(bf16)
+    pl.semaphore_wait(barrier, len(lines))
+    for s, axis in enumerate((0, 2, 3)):
+        peers = stage_peers(here, (axis,))
+        for peer in peers:
+            pl.semaphore_signal(meet_sem.at[s], inc=1, device_id=peer, device_id_type=MESH)
+        if s < 2:
+            place_rank(s, brick_row, rank_row, live, time_row, ray_row, pay, send)
+        pl.semaphore_wait(meet_sem.at[s], len(peers))
+    me = flat(here)
+
+    def go(step, carry):
+        steps = (step // 32, (step // 16) % 2, (step // 4) % 4, step % 4)
+        peer = tuple((v + d) % n for v, d, n in zip(here, steps, SIZES))
+        pltpu.make_async_remote_copy(
+            send.at[flat(peer)], held.at[me], send_sem, recv_sem, device_id=peer, device_id_type=MESH).start()
+        return carry
+
+    lax.fori_loop(1, NDEV, go, 0)
+    held[me] = send[me]
+    rest = pl.ds(0, NDEV - 1)
+    every = pltpu.make_async_remote_copy(
+        send.at[rest], held.at[rest], send_sem, recv_sem, device_id=here, device_id_type=MESH)
+    every.wait_recv()
+    every.wait_send()
+
+
+def place_rank(k, brick_row, rank_row, live, time_row, ray_row, pay, send):
     lanes = iota((128, 128), 1)
-    for k in range(2):
-        picked = jnp.where((target == brick_row) & (rank_row == k) & live, 1.0, 0.0)
-        z, col, w = from_payload(jnp.dot(picked.astype(bf16), pay[...], preferred_element_type=f32))
-        out[:, k, :] = col * 128.0 + z
-        out[:, 2 + k, :] = w
-        value = jnp.sum(picked * time_row, axis=1, keepdims=True)
-        ray = jnp.sum(picked * (ray_row + 1).astype(f32), axis=1, keepdims=True)
-        meta = jnp.where(lanes == k, value, jnp.where(lanes == 2 + k, ray, meta))
-    out[:, 4, :] = meta
+    picked = jnp.where((iota((128, 128), 0).astype(f32) == brick_row) & (rank_row == k) & live, 1.0, 0.0)
+    rows = jnp.dot(picked.astype(bf16), pay[...], preferred_element_type=f32)
+    z, col, w = from_payload(rows)
+    send[:, k, :] = col * 128.0 + z
+    send[:, 2 + k, :] = w
+    value = jnp.sum(picked * time_row, axis=1, keepdims=True)
+    ray = jnp.sum(picked * (ray_row + 1).astype(f32), axis=1, keepdims=True)
+    marks = rows[:, 768:896]
+    if k == 0:
+        send[:, 4, :] = jnp.where(lanes == 0, value, jnp.where(lanes == 2, ray, jnp.where(lanes < 8, marks, 0.0)))
+    else:
+        send[:, 4, :] = jnp.where(lanes == 1, value, jnp.where(lanes == 3, ray, jnp.where(lanes < 8, send[:, 4, :], marks)))
 
 
 def onehot_cols(col_row):
@@ -146,21 +254,13 @@
     return jnp.concatenate([h.reshape(16, 8, 1) for h in halves], axis=1).reshape(SLOTS, 1)
 
 
-def take(x, index):
-    return jnp.take_along_axis(x, index, axis=1, mode="promise_in_bounds")
-
-
-def bucket(n, col, dep, w, bcol, bdep, bw):
-    upto = jnp.where(iota((128, 128), 0) <= iota((128, 128), 1), 1.0, 0.0).astype(bf16)
+def bucket(n, starts, col, dep, w, bcol, bdep, bw):
     rank = iota((SLOTS, 128), 1) & (HALF - 1)
     most = jnp.zeros((SLOTS, 1), i32)
     for b in range(BLOCKS):
-        inside = jnp.where((col >> 8) == b, 1.0, 0.0).astype(bf16)
-        counts = jnp.dot(inside, upto, preferred_element_type=f32).astype(i32)
-        at = jnp.zeros((SLOTS, 128), i32)
-        for step in (64, 32, 16, 8, 4, 2, 1):
-            at = jnp.where(take(counts, at + (step - 1)) <= rank, at + step, at)
-        held = counts[:, 127:128]
+        first = starts[:, b:b + 1]
+        held = (starts[:, b + 1:b + 2] if b + 1 < BLOCKS else SEG) - first
+        at = (first + rank) & (SEG - 1)
         bcol[b] = pair(take(col, at) - b * BLOCK)
         bdep[b] = pair(take(dep, at))
         bw[b] = pair(jnp.where(rank < held, take(w, at), 0.0))
@@ -169,13 +269,12 @@
     return jnp.max(most.astype(f32)).astype(i32)
 
 
-def both_passes(n, most, y_col, col, dep, w, bcol, bdep, bw, extra, q_out, acc, gt, wy, vals, part):
+def both_passes(n, most, y_col, col, dep, w, bcol, bdep, bw, finish_q, q_out, acc, gt, wy, vals, part):
     fits = most <= HALF
 
     def whole():
         q = jnp.concatenate([acc[b, :, 0:128] + acc[b, :, 128:256] for b in range(BLOCKS)], axis=0)
-        if extra is not None:
-            q = q + extra[...]
+        q = finish_q(q)
         q_out[...] = q
         hi, lo = split2(q.T)
         gt[0:128, :] = hi
@@ -225,10 +324,22 @@
     return jnp.sum(place * jnp.concatenate(rows, axis=1), axis=1, keepdims=True)
 
 
+def total_of(x):
+    return jnp.sum(jnp.sum(x, axis=0, keepdims=True), axis=1, keepdims=True)
+
+
+def as_row(values):
+    row = jnp.zeros((8, NDEV), f32)
+    for k, value in enumerate(values):
+        row = jnp.where(iota((8, NDEV), 1) == k, value, row)
+    return row
+
+
 def first_kernel(held, q_out, p_out, col, dep, w, bcol, bdep, bw, info, count, acc, gt, wy, vals, part):
-    meta = held[:, 4, :].T
-    y_row = jnp.concatenate([meta[0:1, :], meta[1:2, :]], axis=1)
-    ray_row = jnp.concatenate([meta[2:3, :], meta[3:4, :]], axis=1).astype(i32) - 1
+    meta = held[:, 4, :]
+    across = meta.T
+    y_row = jnp.concatenate([across[0:1, :], across[1:2, :]], axis=1)
+    ray_row = jnp.concatenate([across[2:3, :], across[3:4, :]], axis=1).astype(i32) - 1
     live = ray_row >= 0
     flags = jnp.broadcast_to(jnp.where(live, 1.0, 0.0), (8, SLOTS)).astype(bf16)
     before = jnp.where(iota((SLOTS, SLOTS), 0) < iota((SLOTS, SLOTS), 1), 1.0, 0.0).astype(bf16)
@@ -239,24 +350,32 @@
     n = jnp.sum(jnp.where(live, 1.0, 0.0)).astype(i32)
     place = place_of(at)
     pay = jnp.concatenate([as_payload(held[:, k, :].astype(i32), held[:, 2 + k, :]) for k in range(2)], axis=0)
-    z, c, lens = from_payload(jnp.dot(place.astype(bf16), pay, preferred_element_type=f32))
+    marks = jnp.concatenate([meta, pltpu.roll(meta, 124, 1)], axis=0).astype(bf16)
+    rows = jnp.dot(place.astype(bf16), jnp.concatenate([pay, marks], axis=1), preferred_element_type=f32)
+    z, c, lens = from_payload(rows)
     col[...] = c.astype(i32)
     dep[...] = z.astype(i32)
     w[...] = lens
-    most = bucket(n, col[...], dep[...], lens, bcol, bdep, bw)
+    most = bucket(n, rows[:, 772:776].astype(i32), col[...], dep[...], lens, bcol, bdep, bw)
     count[0] = n
     count[1] = most
     y_col = jnp.sum(place * y_row, axis=1, keepdims=True)
-    both_passes(n, most, y_col, col, dep, w, bcol, bdep, bw, None, q_out, acc, gt, wy, vals, part)
-    p_out[...] = to_rays(part[...], place_of(at), ray_row)
-
-
-def second_kernel(p, smooth, col, dep, w, bcol, bdep, bw, info, count, q_out, p_out, acc, gt, wy, vals, part):
+    both_passes(n, most, y_col, col, dep, w, bcol, bdep, bw, lambda q: q, q_out, acc, gt, wy, vals, part)
+    p_out[0:RAYS, :] = to_rays(part[...], place_of(at), ray_row)
+    q = q_out[...]
+    p_out[RAYS:RAYS + 8, :] = as_row([total_of(q * q)])
+
+
+def second_kernel(p, shift, q0, smooth, col, dep, w, bcol, bdep, bw, info, count, e_out, p_out, dots, acc, gt, wy, vals,
+                  part):
     place = place_of(info[0:1, :])
     ray_row = info[1:2, :]
     y_col = from_rays(p[...], place, ray_row)
-    both_passes(count[0], count[1], y_col, col, dep, w, bcol, bdep, bw, smooth, q_out, acc, gt, wy, vals, part)
+    finish_q = lambda q: q + smooth[...] - shift[0:1, 0:1] * q0[...]
+    both_passes(count[0], count[1], y_col, col, dep, w, bcol, bdep, bw, finish_q, e_out, acc, gt, wy, vals, part)
     p_out[...] = to_rays(part[...], place, ray_row)
+    e = e_out[...]
+    dots[...] = as_row([total_of(e * q0[...]), total_of(e * e)])
 
 
 def shape(dims, dtype=f32):
@@ -272,48 +391,13 @@
 ]
 
 
-MESH = pl.DeviceIdType.MESH
-SIZES = (4, 2, 4, 4)
 STAGES = ((1, 0), (2,), (3,))
-PEERS = max(len(list(itertools.product(*[range(SIZES[a]) for a in g]))) for g in STAGES) - 1
-
-
-def coords():
-    return tuple(lax.axis_index(a) for a in LON_LAT)
-
-
-def stage_peers(here, group):
-    found = []
-    for steps in itertools.product(*[range(SIZES[a]) for a in group]):
-        if any(steps):
-            add = dict(zip(group, steps))
-            found.append(tuple((v + add.get(i, 0)) % SIZES[i] for i, v in enumerate(here)))
-    return found
-
-
-def ring_peers(here):
-    lon, lat = here[0] * 2 + here[1], here[2] * 4 + here[3]
-    found = []
-    for step in (1, 7):
-        to = (lon + step) % 8
-        found.append((to // 2, to % 2, here[2], here[3]))
-    for step in (1, 15):
-        to = (lat + step) % 16
-        found.append((here[0], here[1], to // 4, to % 4))
-    return found
-
-
-def meet(here):
-    barrier = pltpu.get_barrier_semaphore()
-    peers = [p for g in STAGES for p in stage_peers(here, g)] + ring_peers(here)
-    for peer in peers:
-        pl.semaphore_signal(barrier, inc=1, device_id=peer, device_id_type=MESH)
-    pl.semaphore_wait(barrier, len(peers))
-
-
-def send_stage(s, here, buf, got, send_sem, recv_sem):
+ROUNDS = ((1, 0), (2, 3))
+
+
+def send_stage(s, here, group, buf, got, send_sem, recv_sem):
     copies = []
-    for k, peer in enumerate(stage_peers(here, STAGES[s])):
+    for k, peer in enumerate(stage_peers(here, group)):
         copy = pltpu.make_async_remote_copy(
             buf.at[s], got.at[s, k], send_sem.at[s, k], recv_sem.at[s, k], device_id=peer, device_id_type=MESH)
         copy.start()
@@ -372,14 +456,14 @@
         copy.wait_send()
 
 
-def middle_kernel(p_part, q, p_out, smooth, buf, got, g, edge, halo, send_sem, recv_sem, face_send, face_recv):
+def middle_kernel(p_part, q, p_out, shift, smooth, buf, got, g, edge, halo, send_sem, recv_sem, face_send, face_recv):
     here = coords()
-    meet(here)
+    meet([p for group in STAGES for p in stage_peers(here, group)] + ring_peers(here)[2:])
     buf[0] = p_part[...]
-    first = send_stage(0, here, buf, got, send_sem, recv_sem)
+    first = send_stage(0, here, STAGES[0], buf, got, send_sem, recv_sem)
     faces = send_halo(here, q, edge.at[0], halo.at[0], face_send.at[0], face_recv.at[0])
     buf[1] = add_stage(0, first, buf, got)
-    second = send_stage(1, here, buf, got, send_sem, recv_sem)
+    second = send_stage(1, here, STAGES[1], buf, got, send_sem, recv_sem)
     for copy in faces:
         copy.wait_recv()
 
@@ -389,7 +473,7 @@
     stencil_rows(here, q, halo.at[0], to_g)
     more = send_halo(here, g, edge.at[1], halo.at[1], face_send.at[1], face_recv.at[1])
     buf[2] = add_stage(1, second, buf, got)
-    third = send_stage(2, here, buf, got, send_sem, recv_sem)
+    third = send_stage(2, here, STAGES[2], buf, got, send_sem, recv_sem)
     for copy in more:
         copy.wait_recv()
 
@@ -397,18 +481,20 @@
         smooth[rows, :] = value
 
     stencil_rows(here, g, halo.at[1], to_smooth)
-    p_out[...] = add_stage(2, third, buf, got)
+    total = add_stage(2, third, buf, got)
+    p = total[0:RAYS, :]
+    p_out[...] = p
+    shift[...] = as_row([total_of(p * p) / total[RAYS:RAYS + 1, 0:1], total[RAYS:RAYS + 1, 0:1]])
     finish(first + second + third + faces + more)
 
 
-def last_kernel(count, times, p_part, p0, q0, q1, model, misfit, buf, got, norm, edge, halo, send_sem, recv_sem,
-                face_send, face_recv):
+def last_kernel(count, times, p_part, p0, shift, dots, q0, e, model, misfit, buf, got, small, small_got, norm, edge, halo,
+                send_sem, recv_sem, small_send, small_recv, face_send, face_recv):
     here = coords()
-    meet(here)
-    faces = send_halo(here, q1, edge, halo, face_send, face_recv)
-    buf[0, 0:RAYS, :] = p_part[...]
-    a, b = q0[...], q1[...]
-    dots = [jnp.sum(jnp.sum(x, axis=0, keepdims=True), axis=1, keepdims=True) for x in (a * a, a * b, b * b)]
+    meet([p for group in ROUNDS for p in stage_peers(here, group)])
+    faces = send_halo(here, e, edge, halo, face_send, face_recv)
+    buf[0] = p_part[...]
+    first = send_stage(0, here, STAGES[0], buf, got, send_sem, recv_sem)
     norm[...] = jnp.zeros_like(norm)
     for copy in faces:
         copy.wait_recv()
@@ -416,100 +502,92 @@
     def to_norm(rows, value):
         norm[...] += value * value
 
-    stencil_rows(here, q1, halo, to_norm)
-    dots.append(jnp.sum(jnp.sum(norm[...], axis=0, keepdims=True), axis=1, keepdims=True))
-    lane = iota((8, NDEV), 1)
-    row = jnp.zeros((8, NDEV), f32)
-    for k, dot in enumerate(dots):
-        row = jnp.where(lane == k, dot, row)
-    buf[0, RAYS:RAYS + 8, :] = row
-    sent = []
-    for s in range(len(STAGES)):
-        copies = send_stage(s, here, buf, got, send_sem, recv_sem)
-        total = add_stage(s, copies, buf, got)
-        buf[s + 1] = total
-        sent += copies
-    p1 = total[0:RAYS, :]
-    m0, m1, m2, m3 = [total[RAYS:RAYS + 1, k:k + 1] for k in range(4)]
-    m3 = m3 + jnp.sum(jnp.sum(p1 * p1, axis=0, keepdims=True), axis=1, keepdims=True)
-    r1, r2, r3 = m1 / m0, m2 / m1, m3 / m2
-    c0 = (r3 - r1) / (r3 - r2) / r1
-    c1 = (r1 - r2) / (r3 - r2) / (r1 * r2)
-    model[...] = (SCALE * c0) * a + (SCALE * c1) * b
-    me = ((here[0] * 2 + here[1]) * 4 + here[2]) * 4 + here[3]
-    fit = jnp.where(iota((RAYS, NDEV), 1) == me, c0 * p0[...] + c1 * p1, 0.0)
+    stencil_rows(here, e, halo, to_norm)
+    small[0] = jnp.where(iota((8, NDEV), 1) == 2, total_of(norm[...]), dots[...])
+    one = send_stage(0, here, ROUNDS[0], small, small_got, small_send, small_recv)
+    buf[1] = add_stage(0, first, buf, got)
+    second = send_stage(1, here, STAGES[1], buf, got, send_sem, recv_sem)
+    small[1] = add_stage(0, one, small, small_got)
+    two = send_stage(1, here, ROUNDS[1], small, small_got, small_send, small_recv)
+    buf[2] = add_stage(1, second, buf, got)
+    third = send_stage(2, here, STAGES[2], buf, got, send_sem, recv_sem)
+    moments = add_stage(1, two, small, small_got)
+    pe = add_stage(2, third, buf, got)
+    mu, m0 = shift[0:1, 0:1], shift[0:1, 1:2]
+    s, big = moments[0:1, 0:1] / m0, moments[0:1, 1:2] / m0
+    r = (moments[0:1, 2:3] + total_of(pe * pe)) / m0
+    cross = big + mu * s
+    det = (s + mu) * r - cross * cross
+    a, b = (r - s * cross) / det, (s * s - big) / det
+    model[...] = (SCALE * a) * q0[...] + (SCALE * b) * e[...]
+    fit = jnp.where(iota((RAYS, NDEV), 1) == flat(here), a * p0[...] + b * pe, 0.0)
     column = jnp.sum(fit, axis=1, keepdims=True)
     own = jnp.sum(jnp.where(iota((RAYS, RAYS), 0) == iota((RAYS, RAYS), 1), column, 0.0), axis=0, keepdims=True)
     data = jnp.where(iota((1, RAYS), 1) < count[0], times[...], 0.0)
     misfit[...] = data - own
-    finish(faces + sent)
-
-
-def comm_scratch(rows, faces):
-    return [
-        pltpu.VMEM((len(STAGES) + 1, rows, NDEV), f32),
-        pltpu.VMEM((len(STAGES), PEERS, rows, NDEV), f32),
-    ], [
-        pltpu.VMEM(faces + (2, CLON, DEP), f32),
-        pltpu.VMEM(faces + (4, CLON, DEP), f32),
-        pltpu.SemaphoreType.DMA((len(STAGES), PEERS)),
-        pltpu.SemaphoreType.DMA((len(STAGES), PEERS)),
-        pltpu.SemaphoreType.DMA(faces + (4,)),
-        pltpu.SemaphoreType.DMA(faces + (4,)),
-    ]
+    finish(faces + first + second + third + one + two)
 
 
 def comm_params(number):
     return pltpu.CompilerParams(vmem_limit_bytes=16 << 20, collective_id=number, has_side_effects=True)
 
 
+def face_scratch(*dims):
+    return [pltpu.VMEM(dims + (2, CLON, DEP), f32), pltpu.VMEM(dims + (4, CLON, DEP), f32)]
+
+
+def sems(*dims):
+    return [pltpu.SemaphoreType.DMA(dims), pltpu.SemaphoreType.DMA(dims)]
+
+
 def shards(travel_times, ray_counts, tile_brick, cell_offsets, cell_depths, seg_lengths):
     times = travel_times.reshape(1, RAYS)
-    send = pl.pallas_call(
-        pack_kernel,
+    held = pl.pallas_call(
+        send_kernel,
         out_shape=shape((NDEV, 5, SEG)),
-        in_specs=[SMEM] + [VMEM] * 2 + [pl.BlockSpec(memory_space=pl.ANY)] * 3,
+        in_specs=[SMEM] + [VMEM] * 2 + [pl.BlockSpec(memory_space=pltpu.MemorySpace.HBM)] * 3,
         out_specs=VMEM,
-        scratch_shapes=[pltpu.VMEM((128, 768), bf16)] + [pltpu.VMEM((RAYS, TPR, SEG), d) for d in (i32, i32, f32)]
-        + [pltpu.SemaphoreType.DMA((3,))],
-        compiler_params=PARAMS,
+        scratch_shapes=[pltpu.VMEM((NDEV, 5, SEG), f32), pltpu.VMEM((128, 896), bf16)]
+        + [pltpu.VMEM((RAYS, TPR, SEG), d) for d in (i32, i32, f32)]
+        + [pltpu.SemaphoreType.DMA((3,)), pltpu.SemaphoreType.REGULAR((3,)), pltpu.SemaphoreType.DMA, pltpu.SemaphoreType.DMA],
+        compiler_params=comm_params(2),
     )(ray_counts, tile_brick.T, times, cell_offsets, cell_depths, seg_lengths)
-    held = lax.all_to_all(send, LON_LAT, split_axis=0, concat_axis=0, tiled=True)
     entries = [shape((SLOTS, SEG), d) for d in (i32, i32, f32)] + [shape((BLOCKS, 128, 128), d) for d in (i32, i32, f32)]
     q0, p_part, *lists, info, count = pl.pallas_call(
         first_kernel,
-        out_shape=(shape((COLS, DEP)), shape((RAYS, NDEV)), *entries, shape((2, SLOTS), i32), shape((2,), i32)),
+        out_shape=(shape((COLS, DEP)), shape((RAYS + 8, NDEV)), *entries, shape((2, SLOTS), i32), shape((2,), i32)),
         in_specs=[VMEM],
         out_specs=(VMEM,) * 9 + (SMEM,),
         scratch_shapes=SCRATCH,
         compiler_params=PARAMS,
     )(held)
-    bufs, faces = comm_scratch(RAYS, (2,))
-    p0, smooth = pl.pallas_call(
+    p0, shift, smooth = pl.pallas_call(
         middle_kernel,
-        out_shape=(shape((RAYS, NDEV)), shape((COLS, DEP))),
+        out_shape=(shape((RAYS, NDEV)), shape((8, NDEV)), shape((COLS, DEP))),
         in_specs=[VMEM] * 2,
-        out_specs=(VMEM,) * 2,
-        scratch_shapes=bufs + [pltpu.VMEM((COLS, DEP), f32)] + faces,
+        out_specs=(VMEM,) * 3,
+        scratch_shapes=[pltpu.VMEM((3, RAYS + 8, NDEV), f32), pltpu.VMEM((3, 7, RAYS + 8, NDEV), f32),
+                        pltpu.VMEM((COLS, DEP), f32)] + face_scratch(2) + sems(3, 7) + sems(2, 4),
         compiler_params=comm_params(0),
     )(p_part, q0)
-    q1, p_part = pl.pallas_call(
+    e, p_part, dots = pl.pallas_call(
         second_kernel,
-        out_shape=(shape((COLS, DEP)), shape((RAYS, NDEV))),
-        in_specs=[VMEM] * 9 + [SMEM],
-        out_specs=(VMEM,) * 2,
+        out_shape=(shape((COLS, DEP)), shape((RAYS, NDEV)), shape((8, NDEV))),
+        in_specs=[VMEM] * 11 + [SMEM],
+        out_specs=(VMEM,) * 3,
         scratch_shapes=SCRATCH,
         compiler_params=PARAMS,
-    )(p0, smooth, *lists, info, count)
-    bufs, faces = comm_scratch(RAYS + 8, ())
+    )(p0, shift, q0, smooth, *lists, info, count)
     model, misfit = pl.pallas_call(
         last_kernel,
         out_shape=(shape((COLS, DEP)), shape((1, RAYS))),
-        in_specs=[SMEM] + [VMEM] * 5,
+        in_specs=[SMEM] + [VMEM] * 7,
         out_specs=(VMEM,) * 2,
-        scratch_shapes=bufs + [pltpu.VMEM((CLAT, DEP), f32)] + faces,
+        scratch_shapes=[pltpu.VMEM((3, RAYS, NDEV), f32), pltpu.VMEM((3, 7, RAYS, NDEV), f32),
+                        pltpu.VMEM((2, 8, NDEV), f32), pltpu.VMEM((2, 15, 8, NDEV), f32), pltpu.VMEM((CLAT, DEP), f32)]
+        + face_scratch() + sems(3, 7) + sems(2, 15) + sems(4),
         compiler_params=comm_params(1),
-    )(ray_counts, times, p_part, p0, q0, q1)
+    )(ray_counts, times, p_part, p0, shift, dots, q0, e)
     return (model.reshape(CLON, CLAT, DEP), misfit.reshape(RAYS))
 
 

time: 104 us -> 97.5 us (0.938)
  blocking collectives: 24.6 us -> 0 us
  Pallas kernels: 72.6 us -> 91.4 us
    all_to_all x1 -> x0, blocking collectives: 24.6 us -> none  [shards(): lax.all_to_all(send, LON_LAT, split_axis=0, concat_axis=0, tiled=True)]
    pallas_call x3, Pallas kernels: 37 us -> 56.5 us  [the longest x1 24.5 us: shards(): pl.pallas_call(middle_kernel, out_shape=(shape((RAYS, NDEV)), shape((8, N...]
where the time goes in v4:
time: 97.5 us; the launch traced here: 97.2 us
  Pallas kernels  91.4 us (94%)
  local copies, waits for them, and re-layouts  4.49 us (5%)
  between operations  1.33 us (1%)
    pallas_call x1, Pallas kernels, shards(): pl.pallas_call(last_kernel, out_shape=(shape((COLS, DEP)), shape((1, RAYS...  27.5 us
    pallas_call x1, Pallas kernels, shards(): pl.pallas_call(middle_kernel, out_shape=(shape((RAYS, NDEV)), shape((8, N...  24.5 us
    pallas_call x1, Pallas kernels, shards(): pl.pallas_call(send_kernel, out_shape=shape((NDEV, 5, SEG)), in_specs=[SM...  21.7 us
    pallas_call x1, Pallas kernels, shards(): pl.pallas_call(first_kernel, out_shape=(shape((COLS, DEP)), shape((RAYS +...  10.3 us
    pallas_call x1, Pallas kernels, shards(): pl.pallas_call(second_kernel, out_shape=(shape((COLS, DEP)), shape((RAYS,...  7.44 us
    unnamed x12, local copies, waits for them, and re-layouts  4.49 us

profile of v4, /device:TPU:1, one launch (start us, length us, event | category | flops | bytes accessed | tf_op | source)
XLA Modules:
  0.0 97.2 jit_solution(7161212495556245059)
XLA Ops:
  1.3 0.0 copy-start.4
  1.3 0.0 copy-start.3
  1.3 0.7 copy-done.4
  2.0 0.0 copy-done.3
  2.0 0.0 copy-start
  2.0 0.8 copy-done
  2.8 0.0 copy-start.1
  2.8 0.8 copy-done.1
  3.6 0.0 copy-start.2
  3.6 0.8 copy-done.2
  4.5 21.7 %shard_map.77.held = f32[128,5,128]{2,1,0:T(8,128)S(1)} custom-call(s32[1]{0:T(128)S(6)} %copy.10.count, s32[4,32]{1,0:T(4,128)S(1)} %bitcast.7, f32[1,32]{1,0:T(1,128)S(1)} %bitcast.5, s32[32,4,128]{2,1,0:T(4,128)S(1)} %copy-done, s32[32,4,128]{2,1,0:T(4,128)S(1)} %copy-done.1, f32[32,4,128]{2,1,0:T(4,128)S(1)} %copy-done.2), custom_call_target="tpu_custom_call" | custom-call | tf_op jit(solution)/shard_map/pallas_call | solution.py:545
  26.2 10.3 %shard_map.78 = (f32[1024,128]{1,0:T(8,128)S(1)}, f32[40,128]{1,0:T(8,128)S(1)}, s32[256,128]{1,0:T(8,128)S(1)}, s32[256,128]{1,0:T(8,128)S(1)}, f32[256,128]{1,...) custom-call(f32[128,5,128]{2,1,0:T(8,128)S(1)} %shard_map.77.held), custom_call_target="tpu_custom_call" | custom-call | tf_op jit(solution)/shard_map/pallas_call | solution.py:556
  36.5 24.5 %shard_map.79 = (f32[32,128]{1,0:T(8,128)S(1)}, f32[8,128]{1,0:T(8,128)S(1)}, f32[1024,128]{1,0:T(8,128)S(1)}) custom-call(f32[40,128]{1,0:T(8,128)S(1)} %get-tuple-element.20.p_part, f32[1024,128]{1,0:T(8,128)S(1)} %get-tuple-element.21.q.q0), custom_call_target="tpu_custom_call" | custom-call | tf_op jit(solution)/shard_map/pallas_call | solution.py:564
  61.0 7.4 %shard_map.80 = (f32[1024,128]{1,0:T(8,128)S(1)}, f32[32,128]{1,0:T(8,128)S(1)}, f32[8,128]{1,0:T(8,128)S(1)}) custom-call(f32[32,128]{1,0:T(8,128)S(1)} %get-tuple-element.22.p.p0, f32[8,128]{1,0:T(8,128)S(1)} %get-tuple-element.23.shift, f32[1024,128]{1,0:T(8,128)S(1)} %get-tuple-element.21.q.q0, f32[1024,128]{1,0:T(8,128)S(1)} %get-tuple-element.24.smooth, ...), custom_call_target="tpu_custom_call" | custom-call | tf_op jit(solution)/shard_map/pallas_call | solution.py:573
  68.4 27.5 %shard_map.81 = (f32[1024,128]{1,0:T(8,128)S(1)}, f32[1,32]{1,0:T(1,128)S(1)}) custom-call(s32[1]{0:T(128)S(6)} %copy.10.count, f32[1,32]{1,0:T(1,128)S(1)} %bitcast.6, f32[32,128]{1,0:T(8,128)S(1)} %get-tuple-element.33.p_part, f32[32,128]{1,0:T(8,128)S(1)} %get-tuple-element.22.p.p0, f32[8,128]{1,0:T(8,128)S(1)} %get-tuple-element.23.shift, ...), custom_call_target="tpu_custom_call" | custom-call | tf_op jit(solution)/shard_map/pallas_call | solution.py:581
  95.9 0.8 copy.11
  96.7 0.5 copy.12
Async XLA Ops:
  1.3 0.7 copy-start.4
  1.3 0.7 copy-start.3
  2.0 0.8 copy-start
  2.8 0.8 copy-start.1
  3.6 0.8 copy-start.2

commit v5 on v4

--- a/solution.py
+++ b/solution.py
@@ -433,22 +433,18 @@
     row, lane = iota((CLAT, DEP), 0), iota((CLAT, DEP), 1)
 
     def layer(i, before, after):
-        mine = pl.ds(pl.multiple_of(i * CLAT, CLAT), CLAT)
+        mine = pl.ds(i * CLAT, CLAT)
         f = field[mine, :]
-        lat_before = jnp.where(row == 0, halo[2, pl.ds(i, 1), :] * has_before, pltpu.roll(f, 1, 0))
-        lat_after = jnp.where(row == CLAT - 1, halo[3, pl.ds(i, 1), :] * has_after, pltpu.roll(f, CLAT - 1, 0))
+        lat_before = jnp.where(row == 0, halo[2, i:i + 1, :] * has_before, pltpu.roll(f, 1, 0))
+        lat_after = jnp.where(row == CLAT - 1, halo[3, i:i + 1, :] * has_after, pltpu.roll(f, CLAT - 1, 0))
         up = jnp.where(lane == 0, 0.0, pltpu.roll(f, 1, 1))
         down = jnp.where(lane == DEP - 1, 0.0, pltpu.roll(f, DEP - 1, 1))
         put(mine, DAMP * (6.0 * f - before - after - lat_before - lat_after - up - down))
 
-    def inner(i, carry):
-        layer(i, field[pl.ds(pl.multiple_of((i - 1) * CLAT, CLAT), CLAT), :],
-              field[pl.ds(pl.multiple_of((i + 1) * CLAT, CLAT), CLAT), :])
-        return carry
-
-    layer(0, halo[0], field[CLAT:2 * CLAT, :])
-    layer(CLON - 1, field[COLS - 2 * CLAT:COLS - CLAT, :], halo[1])
-    lax.fori_loop(1, CLON - 1, inner, 0)
+    for i in range(CLON):
+        before = field[(i - 1) * CLAT:i * CLAT, :] if i else halo[0]
+        after = field[(i + 1) * CLAT:(i + 2) * CLAT, :] if i < CLON - 1 else halo[1]
+        layer(i, before, after)
 
 
 def finish(copies):
@@ -528,8 +524,8 @@
     finish(faces + first + second + third + one + two)
 
 
-def comm_params(number):
-    return pltpu.CompilerParams(vmem_limit_bytes=16 << 20, collective_id=number, has_side_effects=True)
+def comm_params(number, room=16 << 20):
+    return pltpu.CompilerParams(vmem_limit_bytes=room, collective_id=number, has_side_effects=True)
 
 
 def face_scratch(*dims):
@@ -550,7 +546,7 @@
         scratch_shapes=[pltpu.VMEM((NDEV, 5, SEG), f32), pltpu.VMEM((128, 896), bf16)]
         + [pltpu.VMEM((RAYS, TPR, SEG), d) for d in (i32, i32, f32)]
         + [pltpu.SemaphoreType.DMA((3,)), pltpu.SemaphoreType.REGULAR((3,)), pltpu.SemaphoreType.DMA, pltpu.SemaphoreType.DMA],
-        compiler_params=comm_params(2),
+        compiler_params=comm_params(2, 60 << 20),
     )(ray_counts, tile_brick.T, times, cell_offsets, cell_depths, seg_lengths)
     entries = [shape((SLOTS, SEG), d) for d in (i32, i32, f32)] + [shape((BLOCKS, 128, 128), d) for d in (i32, i32, f32)]
     q0, p_part, *lists, info, count = pl.pallas_call(

time: 97.5 us -> 90.3 us (0.926)
  Pallas kernels: 91.4 us -> 85.5 us
  local copies, waits for them, and re-layouts: 4.49 us -> 3 us
    pallas_call x1, Pallas kernels: 27.5 us -> 23.8 us  [shards(): pl.pallas_call(last_kernel, out_shape=(shape((COLS, DEP)), shape((1, RAYS...]
    pallas_call x1, Pallas kernels: 24.5 us -> 21.1 us  [shards(): pl.pallas_call(middle_kernel, out_shape=(shape((RAYS, NDEV)), shape((8, N...]
    unnamed x12 -> x6, local copies, waits for them, and re-layouts: 4.49 us -> 3 us
    pallas_call x1, Pallas kernels: 21.7 us -> 22.9 us  [shards(): pl.pallas_call(send_kernel, out_shape=shape((NDEV, 5, SEG)), in_specs=[SM...]
where the time goes in v5:
time: 90.3 us; the launch traced here: 89.9 us
  Pallas kernels  85.5 us (95%)
  local copies, waits for them, and re-layouts  3 us (3%)
  between operations  1.32 us (1%)
    pallas_call x1, Pallas kernels, shards(): pl.pallas_call(last_kernel, out_shape=(shape((COLS, DEP)), shape((1, RAYS...  23.8 us
    pallas_call x1, Pallas kernels, shards(): pl.pallas_call(send_kernel, out_shape=shape((NDEV, 5, SEG)), in_specs=[SM...  22.9 us
    pallas_call x1, Pallas kernels, shards(): pl.pallas_call(middle_kernel, out_shape=(shape((RAYS, NDEV)), shape((8, N...  21.1 us
    pallas_call x1, Pallas kernels, shards(): pl.pallas_call(first_kernel, out_shape=(shape((COLS, DEP)), shape((RAYS +...  10.3 us
    pallas_call x1, Pallas kernels, shards(): pl.pallas_call(second_kernel, out_shape=(shape((COLS, DEP)), shape((RAYS,...  7.43 us
    unnamed x6, local copies, waits for them, and re-layouts  3 us

profile of v5, /device:TPU:1, one launch (start us, length us, event | category | flops | bytes accessed | tf_op | source)
XLA Modules:
  0.0 89.9 jit_solution(4942935177636093041)
XLA Ops:
  1.3 22.9 %shard_map.77.held = f32[128,5,128]{2,1,0:T(8,128)} custom-call(s32[1]{0:T(128)S(6)} %copy.10.count, s32[4,32]{1,0:T(4,128)} %bitcast.8, f32[1,32]{1,0:T(1,128)} %bitcast.5, s32[32,4,128]{2,1,0:T(4,128)} %offs_in.1, s32[32,4,128]{2,1,0:T(4,128)} %deps_in.1, f32[32,4,128]{2,1,0:T(4,128)} %lens_in.1), custom_call_target="tpu_custom_call" | custom-call | tf_op jit(solution)/shard_map/pallas_call | solution.py:541
  24.1 0.0 copy-start
  24.2 1.0 %copy-done = f32[128,5,128]{2,1,0:T(8,128)S(1)} copy-done((f32[128,5,128]{2,1,0:T(8,128)S(1)}, f32[128,5,128]{2,1,0:T(8,128)}, u32[]{:S(2)}) %copy-start) | copy-done | bytes 327704
  25.2 10.3 %shard_map.78 = (f32[1024,128]{1,0:T(8,128)S(1)}, f32[40,128]{1,0:T(8,128)S(1)}, s32[256,128]{1,0:T(8,128)S(1)}, s32[256,128]{1,0:T(8,128)S(1)}, f32[256,128]{1,...) custom-call(f32[128,5,128]{2,1,0:T(8,128)S(1)} %copy-done), custom_call_target="tpu_custom_call" | custom-call | tf_op jit(solution)/shard_map/pallas_call | solution.py:552
  35.5 21.1 %shard_map.79 = (f32[32,128]{1,0:T(8,128)S(1)}, f32[8,128]{1,0:T(8,128)S(1)}, f32[1024,128]{1,0:T(8,128)S(1)}) custom-call(f32[40,128]{1,0:T(8,128)S(1)} %get-tuple-element.20.p_part, f32[1024,128]{1,0:T(8,128)S(1)} %get-tuple-element.21.q.q0), custom_call_target="tpu_custom_call" | custom-call | tf_op jit(solution)/shard_map/pallas_call | solution.py:560
  56.6 7.4 %shard_map.80 = (f32[1024,128]{1,0:T(8,128)S(1)}, f32[32,128]{1,0:T(8,128)S(1)}, f32[8,128]{1,0:T(8,128)S(1)}) custom-call(f32[32,128]{1,0:T(8,128)S(1)} %get-tuple-element.22.p.p0, f32[8,128]{1,0:T(8,128)S(1)} %get-tuple-element.23.shift, f32[1024,128]{1,0:T(8,128)S(1)} %get-tuple-element.21.q.q0, f32[1024,128]{1,0:T(8,128)S(1)} %get-tuple-element.24.smooth, ...), custom_call_target="tpu_custom_call" | custom-call | tf_op jit(solution)/shard_map/pallas_call | solution.py:569
  64.0 0.0 copy-start.1
  64.0 0.7 copy-done.1
  64.7 23.8 %shard_map.81 = (f32[1024,128]{1,0:T(8,128)S(1)}, f32[1,32]{1,0:T(1,128)S(1)}) custom-call(s32[1]{0:T(128)S(6)} %copy.10.count, f32[1,32]{1,0:T(1,128)S(1)} %bitcast.6, f32[32,128]{1,0:T(8,128)S(1)} %get-tuple-element.33.p_part, f32[32,128]{1,0:T(8,128)S(1)} %get-tuple-element.22.p.p0, f32[8,128]{1,0:T(8,128)S(1)} %get-tuple-element.23.shift, ...), custom_call_target="tpu_custom_call" | custom-call | tf_op jit(solution)/shard_map/pallas_call | solution.py:577
  88.5 0.8 copy.11
  89.3 0.5 copy.12
Async XLA Ops:
  24.1 1.0 %copy-start = (f32[128,5,128]{2,1,0:T(8,128)S(1)}, f32[128,5,128]{2,1,0:T(8,128)}, u32[]{:S(2)}) copy-start(f32[128,5,128]{2,1,0:T(8,128)} %shard_map.77.held) | copy-start | bytes 983044
  64.0 0.7 copy-start.1

commit v6 on v5

--- a/solution.py
+++ b/solution.py
@@ -14,7 +14,9 @@
 NDEV = 128
 SLOTS = 2 * NDEV
 CHUNK = 8
-BLOCKS, BLOCK, HALF = 4, 256, 64
+BLOCKS, BLOCK = 4, 256
+GROUPS, SHARE = 6, 6
+TILES, PLACES, ROWS = 8 * SHARE, 8 * SHARE * GROUPS, 16 * GROUPS
 SCALE = 8.0
 DAMP = 0.01 * SCALE
 LON_LAT = ("lon_0", "lon_1", "lat_0", "lat_1")
@@ -227,7 +229,6 @@
 
     def body(c, carry):
         rows = [pl.ds(c * CHUNK + j, 1) for j in range(CHUNK)]
-        sums = [jnp.zeros((8, 128), f32)] * CHUNK
         for b in range(BLOCKS):
             right = jnp.concatenate([onehot_cols(col(b, r)) for r in rows], axis=1)
             res = jnp.dot(gt[:, b * BLOCK:(b + 1) * BLOCK], right, preferred_element_type=f32)
@@ -235,46 +236,74 @@
                 at = slice(j * 128, (j + 1) * 128)
                 both = res[0:128, at] + res[128:256, at]
                 here = jnp.where(iota((DEP, 128), 0) == dep(b, r), both, 0.0)
-                sums[j] = sums[j] + here.reshape(16, 8, 128).sum(axis=0) * w(b, r)
-        for j, r in enumerate(rows):
-            out[r, :] = jnp.sum(sums[j], axis=0, keepdims=True)
+                out[b, r, :] = jnp.sum(here, axis=0, keepdims=True) * w(b, r)
         return carry
 
     lax.fori_loop(0, chunks, body, 0)
 
 
-def pair(x):
-    x = x.reshape(16, 16, 128)
-    return jnp.where(iota((16, 8, 128), 2) < HALF, x[:, 0:8], x[:, 8:16]).reshape(128, 128)
-
-
-def unpair(x):
-    low = iota((128, 128), 1) < HALF
-    halves = [jnp.sum(jnp.where(m, x, 0.0), axis=1, keepdims=True) for m in (low, ~low)]
-    return jnp.concatenate([h.reshape(16, 8, 1) for h in halves], axis=1).reshape(SLOTS, 1)
-
-
-def bucket(n, starts, col, dep, w, bcol, bdep, bw):
-    rank = iota((SLOTS, 128), 1) & (HALF - 1)
-    most = jnp.zeros((SLOTS, 1), i32)
+def bucket(n, starts, cell, w, bcol, bdep, bw, btile):
+    alive = iota((PLACES, 1), 0) < n
+    group = iota((GROUPS, 8, 1), 0)
+    last = (n - 1) // TILES
+    cells = cell.reshape(GROUPS, SHARE, 8, 128)
+    ws = w.reshape(GROUPS, SHARE, 8, 128)
+    most = jnp.zeros((GROUPS, 8, 1), i32)
     for b in range(BLOCKS):
         first = starts[:, b:b + 1]
-        held = (starts[:, b + 1:b + 2] if b + 1 < BLOCKS else SEG) - first
-        at = (first + rank) & (SEG - 1)
-        bcol[b] = pair(take(col, at) - b * BLOCK)
-        bdep[b] = pair(take(dep, at))
-        bw[b] = pair(jnp.where(rank < held, take(w, at), 0.0))
-        most = jnp.maximum(most, held)
-    most = jnp.where(iota((SLOTS, 1), 0) < n, most, 0)
-    return jnp.max(most.astype(f32)).astype(i32)
-
-
-def both_passes(n, most, y_col, col, dep, w, bcol, bdep, bw, finish_q, q_out, acc, gt, wy, vals, part):
-    fits = most <= HALF
+        held = jnp.where(alive, (starts[:, b + 1:b + 2] if b + 1 < BLOCKS else SEG) - first, 0)
+        first, held = first.reshape(GROUPS, SHARE, 8, 1), held.reshape(GROUPS, SHARE, 8, 1)
+        for h in range(2):
+            spot = iota((GROUPS, 8, 128), 2) + h * 128
+            before = jnp.zeros((GROUPS, 8, 1), i32)
+            own_cell, own_w = jnp.zeros((GROUPS, 8, 128), i32), jnp.zeros((GROUPS, 8, 128), f32)
+            tile = jnp.zeros((GROUPS, 8, 128), i32)
+            for k in range(SHARE):
+                at = ((first[:, k] + spot - before) & (SEG - 1)).reshape(GROUPS * 8, 128)
+                mine = spot >= before
+                own_cell = jnp.where(mine, take(cells[:, k].reshape(GROUPS * 8, 128), at).reshape(GROUPS, 8, 128), own_cell)
+                own_w = jnp.where(mine, take(ws[:, k].reshape(GROUPS * 8, 128), at).reshape(GROUPS, 8, 128), own_w)
+                tile = jnp.where(mine, k, tile)
+                before = before + held[:, k]
+            own_w = jnp.where(spot < before, own_w, 0.0)
+            for g in range(GROUPS):
+                rows = slice(g * 16 + h * 8, g * 16 + h * 8 + 8)
+                bcol[b, rows, :] = (own_cell[g] >> 7) - b * BLOCK
+                bdep[b, rows, :] = own_cell[g] & 127
+                bw[b, rows, :] = own_w[g]
+                btile[b, rows, :] = tile[g]
+        most = jnp.maximum(most, before)
+    ending = jnp.max(jnp.where(group == last, most, 0).astype(f32)).astype(i32)
+    chunks = 2 * (last + 1) - jnp.where(ending <= 128, 1, 0)
+    return jnp.max(most.astype(f32)).astype(i32), jnp.where(n > 0, chunks, 0)
+
+
+def per_entry(y_col, tile):
+    y = y_col.reshape(GROUPS, SHARE, 8, 1)
+    tile = tile.reshape(GROUPS, 2, 8, 128)
+    spread = jnp.zeros((GROUPS, 2, 8, 128), f32)
+    for k in range(SHARE):
+        spread = jnp.where(tile == k, y[:, k:k + 1], spread)
+    return spread.reshape(ROWS, 128)
+
+
+def per_tile(vals, btile):
+    sums = [jnp.zeros((GROUPS, 8, 128), f32)] * SHARE
+    for b in range(BLOCKS):
+        value = vals[b, 0:ROWS, :].reshape(GROUPS, 2, 8, 128)
+        tile = btile[b].reshape(GROUPS, 2, 8, 128)
+        for k in range(SHARE):
+            mine = jnp.where(tile == k, value, 0.0)
+            sums[k] = sums[k] + mine[:, 0] + mine[:, 1]
+    columns = [jnp.sum(x, axis=2, keepdims=True)[:, None] for x in sums]
+    return jnp.concatenate(columns, axis=1).reshape(PLACES, 1)
+
+
+def both_passes(count, y_col, cell, w, bcol, bdep, bw, btile, finish_q, q_out, acc, gt, wy, vals, part):
+    fits = count[1] <= 256
 
     def whole():
-        q = jnp.concatenate([acc[b, :, 0:128] + acc[b, :, 128:256] for b in range(BLOCKS)], axis=0)
-        q = finish_q(q)
+        q = finish_q(jnp.concatenate([acc[b, :, 0:128] + acc[b, :, 128:256] for b in range(BLOCKS)], axis=0))
         q_out[...] = q
         hi, lo = split2(q.T)
         gt[0:128, :] = hi
@@ -282,29 +311,27 @@
 
     @pl.when(fits)
     def _():
-        chunks = (n + 2 * CHUNK - 1) // (2 * CHUNK)
-        y = pair(jnp.broadcast_to(y_col, (SLOTS, 128)))
         for b in range(BLOCKS):
-            wy[b] = bw[b] * y
+            wy[b, 0:ROWS, :] = bw[b] * per_entry(y_col, btile[b])
         cols, deps = (lambda b, r: bcol[b, r, :]), (lambda b, r: bdep[b, r, :])
-        scatter_rows(acc, chunks, cols, deps, lambda b, r: wy[b, r, :])
+        scatter_rows(acc, count[2], cols, deps, lambda b, r: wy[b, r, :])
         whole()
-        gather_rows(gt, chunks, cols, deps, lambda b, r: bw[b, r, :], vals.at[pl.ds(0, 128)])
-        part[...] = unpair(vals[0:128, :])
+        gather_rows(gt, count[2], cols, deps, lambda b, r: bw[b, r, :], vals)
+        part[...] = per_tile(vals, btile)
 
     @pl.when(jnp.logical_not(fits))
     def _():
-        chunks = (n + CHUNK - 1) // CHUNK
-        vals[...] = w[...] * y_col
-        cols, deps = (lambda b, r: col[r, :] - b * BLOCK), (lambda b, r: dep[r, :])
-        scatter_rows(acc, chunks, cols, deps, lambda b, r: vals[r, :])
+        chunks = (count[0] + CHUNK - 1) // CHUNK
+        wy[0] = w[...] * y_col
+        cols, deps = (lambda b, r: (cell[r, :] >> 7) - b * BLOCK), (lambda b, r: cell[r, :] & 127)
+        scatter_rows(acc, chunks, cols, deps, lambda b, r: wy[0, r, :])
         whole()
         gather_rows(gt, chunks, cols, deps, lambda b, r: w[r, :], vals)
-        part[...] = jnp.sum(vals[...], axis=1, keepdims=True)
+        part[...] = jnp.sum((vals[0] + vals[1]) + (vals[2] + vals[3]), axis=1, keepdims=True)
 
 
 def place_of(slot_info):
-    return jnp.where(iota((SLOTS, SLOTS), 0) == slot_info, 1.0, 0.0)
+    return jnp.where(iota((PLACES, SLOTS), 0) == slot_info, 1.0, 0.0)
 
 
 def to_rays(partial, place, rays):
@@ -335,7 +362,7 @@
     return row
 
 
-def first_kernel(held, q_out, p_out, col, dep, w, bcol, bdep, bw, info, count, acc, gt, wy, vals, part):
+def first_kernel(held, q_out, p_out, cell, w, bcol, bdep, bw, btile, info, count, acc, gt, wy, vals, part):
     meta = held[:, 4, :]
     across = meta.T
     y_row = jnp.concatenate([across[0:1, :], across[1:2, :]], axis=1)
@@ -353,26 +380,26 @@
     marks = jnp.concatenate([meta, pltpu.roll(meta, 124, 1)], axis=0).astype(bf16)
     rows = jnp.dot(place.astype(bf16), jnp.concatenate([pay, marks], axis=1), preferred_element_type=f32)
     z, c, lens = from_payload(rows)
-    col[...] = c.astype(i32)
-    dep[...] = z.astype(i32)
+    cell[...] = (c * 128.0 + z).astype(i32)
     w[...] = lens
-    most = bucket(n, rows[:, 772:776].astype(i32), col[...], dep[...], lens, bcol, bdep, bw)
+    most, chunks = bucket(n, rows[:, 772:776].astype(i32), cell[...], lens, bcol, bdep, bw, btile)
     count[0] = n
     count[1] = most
+    count[2] = chunks
     y_col = jnp.sum(place * y_row, axis=1, keepdims=True)
-    both_passes(n, most, y_col, col, dep, w, bcol, bdep, bw, lambda q: q, q_out, acc, gt, wy, vals, part)
+    both_passes(count, y_col, cell, w, bcol, bdep, bw, btile, lambda q: q, q_out, acc, gt, wy, vals, part)
     p_out[0:RAYS, :] = to_rays(part[...], place_of(at), ray_row)
     q = q_out[...]
     p_out[RAYS:RAYS + 8, :] = as_row([total_of(q * q)])
 
 
-def second_kernel(p, shift, q0, smooth, col, dep, w, bcol, bdep, bw, info, count, e_out, p_out, dots, acc, gt, wy, vals,
+def second_kernel(p, shift, q0, smooth, cell, w, bcol, bdep, bw, btile, info, count, e_out, p_out, dots, acc, gt, wy, vals,
                   part):
     place = place_of(info[0:1, :])
     ray_row = info[1:2, :]
     y_col = from_rays(p[...], place, ray_row)
     finish_q = lambda q: q + smooth[...] - shift[0:1, 0:1] * q0[...]
-    both_passes(count[0], count[1], y_col, col, dep, w, bcol, bdep, bw, finish_q, e_out, acc, gt, wy, vals, part)
+    both_passes(count, y_col, cell, w, bcol, bdep, bw, btile, finish_q, e_out, acc, gt, wy, vals, part)
     p_out[...] = to_rays(part[...], place, ray_row)
     e = e_out[...]
     dots[...] = as_row([total_of(e * q0[...]), total_of(e * e)])
@@ -385,9 +412,9 @@
 SCRATCH = [
     pltpu.VMEM((BLOCKS, BLOCK, 256), f32),
     pltpu.VMEM((256, COLS), bf16),
-    pltpu.VMEM((BLOCKS, 128, 128), f32),
-    pltpu.VMEM((SLOTS, SEG), f32),
-    pltpu.VMEM((SLOTS, 1), f32),
+    pltpu.VMEM((BLOCKS, PLACES, SEG), f32),
+    pltpu.VMEM((BLOCKS, PLACES, SEG), f32),
+    pltpu.VMEM((PLACES, 1), f32),
 ]
 
 
@@ -548,10 +575,10 @@
         + [pltpu.SemaphoreType.DMA((3,)), pltpu.SemaphoreType.REGULAR((3,)), pltpu.SemaphoreType.DMA, pltpu.SemaphoreType.DMA],
         compiler_params=comm_params(2, 60 << 20),
     )(ray_counts, tile_brick.T, times, cell_offsets, cell_depths, seg_lengths)
-    entries = [shape((SLOTS, SEG), d) for d in (i32, i32, f32)] + [shape((BLOCKS, 128, 128), d) for d in (i32, i32, f32)]
+    entries = [shape((PLACES, SEG), d) for d in (i32, f32)] + [shape((BLOCKS, ROWS, 128), d) for d in (i32, i32, f32, i32)]
     q0, p_part, *lists, info, count = pl.pallas_call(
         first_kernel,
-        out_shape=(shape((COLS, DEP)), shape((RAYS + 8, NDEV)), *entries, shape((2, SLOTS), i32), shape((2,), i32)),
+        out_shape=(shape((COLS, DEP)), shape((RAYS + 8, NDEV)), *entries, shape((2, SLOTS), i32), shape((3,), i32)),
         in_specs=[VMEM],
         out_specs=(VMEM,) * 9 + (SMEM,),
         scratch_shapes=SCRATCH,

time: 90.3 us -> 85.5 us (0.947)
  Pallas kernels: 85.5 us -> 80.9 us
    pallas_call x1, Pallas kernels: 21.1 us -> 18.7 us  [shards(): pl.pallas_call(middle_kernel, out_shape=(shape((RAYS, NDEV)), shape((8, N...]
    pallas_call x1, Pallas kernels: 7.43 us -> 6.1 us  [shards(): pl.pallas_call(second_kernel, out_shape=(shape((COLS, DEP)), shape((RAYS,...]
where the time goes in v6:
time: 85.5 us; the launch traced here: 85.2 us
  Pallas kernels  80.9 us (95%)
  local copies, waits for them, and re-layouts  3 us (4%)
  between operations  1.32 us (2%)
    pallas_call x1, Pallas kernels, shards(): pl.pallas_call(last_kernel, out_shape=(shape((COLS, DEP)), shape((1, RAYS...  23.1 us
    pallas_call x1, Pallas kernels, shards(): pl.pallas_call(send_kernel, out_shape=shape((NDEV, 5, SEG)), in_specs=[SM...  22.9 us
    pallas_call x1, Pallas kernels, shards(): pl.pallas_call(middle_kernel, out_shape=(shape((RAYS, NDEV)), shape((8, N...  18.7 us
    pallas_call x1, Pallas kernels, shards(): pl.pallas_call(first_kernel, out_shape=(shape((COLS, DEP)), shape((RAYS +...  10.1 us
    pallas_call x1, Pallas kernels, shards(): pl.pallas_call(second_kernel, out_shape=(shape((COLS, DEP)), shape((RAYS,...  6.1 us
    unnamed x6, local copies, waits for them, and re-layouts  3 us

profile of v6, /device:TPU:1, one launch (start us, length us, event | category | flops | bytes accessed | tf_op | source)
XLA Modules:
  0.0 85.2 jit_solution(10006495027312579793)
XLA Ops:
  1.3 22.9 %shard_map.77.held = f32[128,5,128]{2,1,0:T(8,128)} custom-call(s32[1]{0:T(128)S(6)} %copy.10.count, s32[4,32]{1,0:T(4,128)} %bitcast.8, f32[1,32]{1,0:T(1,128)} %bitcast.5, s32[32,4,128]{2,1,0:T(4,128)} %offs_in.1, s32[32,4,128]{2,1,0:T(4,128)} %deps_in.1, f32[32,4,128]{2,1,0:T(4,128)} %lens_in.1), custom_call_target="tpu_custom_call" | custom-call | tf_op jit(solution)/shard_map/pallas_call | solution.py:568
  24.1 0.0 copy-start
  24.2 1.0 %copy-done = f32[128,5,128]{2,1,0:T(8,128)S(1)} copy-done((f32[128,5,128]{2,1,0:T(8,128)S(1)}, f32[128,5,128]{2,1,0:T(8,128)}, u32[]{:S(2)}) %copy-start) | copy-done | bytes 327704
  25.2 10.1 %shard_map.78 = (f32[1024,128]{1,0:T(8,128)S(1)}, f32[40,128]{1,0:T(8,128)S(1)}, s32[288,128]{1,0:T(8,128)S(1)}, f32[288,128]{1,0:T(8,128)S(1)}, s32[4,96,128]{2...) custom-call(f32[128,5,128]{2,1,0:T(8,128)S(1)} %copy-done), custom_call_target="tpu_custom_call" | custom-call | tf_op jit(solution)/shard_map/pallas_call | solution.py:579
  35.3 18.7 %shard_map.79 = (f32[32,128]{1,0:T(8,128)S(1)}, f32[8,128]{1,0:T(8,128)S(1)}, f32[1024,128]{1,0:T(8,128)S(1)}) custom-call(f32[40,128]{1,0:T(8,128)S(1)} %get-tuple-element.20.p_part, f32[1024,128]{1,0:T(8,128)S(1)} %get-tuple-element.21.q.q0), custom_call_target="tpu_custom_call" | custom-call | tf_op jit(solution)/shard_map/pallas_call | solution.py:587
  54.0 6.1 %shard_map.80 = (f32[1024,128]{1,0:T(8,128)S(1)}, f32[32,128]{1,0:T(8,128)S(1)}, f32[8,128]{1,0:T(8,128)S(1)}) custom-call(f32[32,128]{1,0:T(8,128)S(1)} %get-tuple-element.22.p.p0, f32[8,128]{1,0:T(8,128)S(1)} %get-tuple-element.23.shift, f32[1024,128]{1,0:T(8,128)S(1)} %get-tuple-element.21.q.q0, f32[1024,128]{1,0:T(8,128)S(1)} %get-tuple-element.24.smooth, ...), custom_call_target="tpu_custom_call" | custom-call | tf_op jit(solution)/shard_map/pallas_call | solution.py:596
  60.1 0.0 copy-start.1
  60.2 0.7 copy-done.1
  60.8 23.1 %shard_map.81 = (f32[1024,128]{1,0:T(8,128)S(1)}, f32[1,32]{1,0:T(1,128)S(1)}) custom-call(s32[1]{0:T(128)S(6)} %copy.10.count, f32[1,32]{1,0:T(1,128)S(1)} %bitcast.6, f32[32,128]{1,0:T(8,128)S(1)} %get-tuple-element.33.p_part, f32[32,128]{1,0:T(8,128)S(1)} %get-tuple-element.22.p.p0, f32[8,128]{1,0:T(8,128)S(1)} %get-tuple-element.23.shift, ...), custom_call_target="tpu_custom_call" | custom-call | tf_op jit(solution)/shard_map/pallas_call | solution.py:604
  83.9 0.8 copy.11
  84.7 0.5 copy.12
Async XLA Ops:
  24.1 1.0 %copy-start = (f32[128,5,128]{2,1,0:T(8,128)S(1)}, f32[128,5,128]{2,1,0:T(8,128)}, u32[]{:S(2)}) copy-start(f32[128,5,128]{2,1,0:T(8,128)} %shard_map.77.held) | copy-start | bytes 983044
  60.1 0.7 copy-start.1

commit v7 on v6

--- a/solution.py
+++ b/solution.py
@@ -243,39 +243,45 @@
 
 
 def bucket(n, starts, cell, w, bcol, bdep, bw, btile):
-    alive = iota((PLACES, 1), 0) < n
-    group = iota((GROUPS, 8, 1), 0)
-    last = (n - 1) // TILES
-    cells = cell.reshape(GROUPS, SHARE, 8, 128)
-    ws = w.reshape(GROUPS, SHARE, 8, 128)
-    most = jnp.zeros((GROUPS, 8, 1), i32)
-    for b in range(BLOCKS):
-        first = starts[:, b:b + 1]
-        held = jnp.where(alive, (starts[:, b + 1:b + 2] if b + 1 < BLOCKS else SEG) - first, 0)
-        first, held = first.reshape(GROUPS, SHARE, 8, 1), held.reshape(GROUPS, SHARE, 8, 1)
-        for h in range(2):
-            spot = iota((GROUPS, 8, 128), 2) + h * 128
-            before = jnp.zeros((GROUPS, 8, 1), i32)
-            own_cell, own_w = jnp.zeros((GROUPS, 8, 128), i32), jnp.zeros((GROUPS, 8, 128), f32)
-            tile = jnp.zeros((GROUPS, 8, 128), i32)
+    groups = (n + TILES - 1) // TILES
+    lane = iota((8, 128), 1)
+
+    def body(g, carry):
+        most, _ = carry
+        rows = [pl.ds(pl.multiple_of(g * TILES + 8 * k, 8), 8) for k in range(SHARE)]
+        cells, ws = [cell[r, :] for r in rows], [w[r, :] for r in rows]
+        firsts = [[jnp.broadcast_to(starts[r, 4 + b:5 + b], (8, 128)) for b in range(BLOCKS)] for r in rows]
+        alive = [iota((8, 128), 0) + (g * TILES + 8 * k) < n for k in range(SHARE)]
+        ending = jnp.zeros((8, 128), f32)
+        for b in range(BLOCKS):
+            before = [jnp.zeros((8, 128), f32)]
             for k in range(SHARE):
-                at = ((first[:, k] + spot - before) & (SEG - 1)).reshape(GROUPS * 8, 128)
-                mine = spot >= before
-                own_cell = jnp.where(mine, take(cells[:, k].reshape(GROUPS * 8, 128), at).reshape(GROUPS, 8, 128), own_cell)
-                own_w = jnp.where(mine, take(ws[:, k].reshape(GROUPS * 8, 128), at).reshape(GROUPS, 8, 128), own_w)
-                tile = jnp.where(mine, k, tile)
-                before = before + held[:, k]
-            own_w = jnp.where(spot < before, own_w, 0.0)
-            for g in range(GROUPS):
-                rows = slice(g * 16 + h * 8, g * 16 + h * 8 + 8)
-                bcol[b, rows, :] = (own_cell[g] >> 7) - b * BLOCK
-                bdep[b, rows, :] = own_cell[g] & 127
-                bw[b, rows, :] = own_w[g]
-                btile[b, rows, :] = tile[g]
-        most = jnp.maximum(most, before)
-    ending = jnp.max(jnp.where(group == last, most, 0).astype(f32)).astype(i32)
-    chunks = 2 * (last + 1) - jnp.where(ending <= 128, 1, 0)
-    return jnp.max(most.astype(f32)).astype(i32), jnp.where(n > 0, chunks, 0)
+                after = firsts[k][b + 1] if b + 1 < BLOCKS else float(SEG)
+                before.append(before[-1] + jnp.where(alive[k], after - firsts[k][b], 0.0))
+            for h in range(2):
+                spot = lane + h * 128
+                own_cell, own_w = jnp.zeros((8, 128), i32), jnp.zeros((8, 128), f32)
+                tile = jnp.zeros((8, 128), i32)
+                for k in range(SHARE):
+                    start = before[k].astype(i32)
+                    at = (firsts[k][b].astype(i32) - start + spot) & (SEG - 1)
+                    mine = spot >= start
+                    own_cell = jnp.where(mine, take(cells[k], at), own_cell)
+                    own_w = jnp.where(mine, take(ws[k], at), own_w)
+                    tile = jnp.where(mine, k, tile)
+                own_w = jnp.where(spot < before[SHARE].astype(i32), own_w, 0.0)
+                out = pl.ds(pl.multiple_of(g * 16 + h * 8, 8), 8)
+                bcol[b, out, :] = (own_cell >> 7) - b * BLOCK
+                bdep[b, out, :] = own_cell & 127
+                bw[b, out, :] = own_w
+                btile[b, out, :] = tile
+            ending = jnp.maximum(ending, before[SHARE])
+        return jnp.maximum(most, ending), ending
+
+    none = jnp.zeros((8, 128), f32)
+    most, ending = lax.fori_loop(0, groups, body, (none, none))
+    chunks = 2 * groups - jnp.where(jnp.max(ending) <= 128.0, 1, 0)
+    return jnp.max(most).astype(i32), jnp.where(n > 0, chunks, 0)
 
 
 def per_entry(y_col, tile):
@@ -362,7 +368,9 @@
     return row
 
 
-def first_kernel(held, q_out, p_out, cell, w, bcol, bdep, bw, btile, info, count, acc, gt, wy, vals, part):
+def first_kernel(held, times, q_out, p_out, times_out, cell, w, bcol, bdep, bw, btile, info, count, acc, gt, wy, vals, part,
+                 starts):
+    times_out[...] = times[...]
     meta = held[:, 4, :]
     across = meta.T
     y_row = jnp.concatenate([across[0:1, :], across[1:2, :]], axis=1)
@@ -382,7 +390,8 @@
     z, c, lens = from_payload(rows)
     cell[...] = (c * 128.0 + z).astype(i32)
     w[...] = lens
-    most, chunks = bucket(n, rows[:, 772:776].astype(i32), cell[...], lens, bcol, bdep, bw, btile)
+    starts[...] = rows[:, 768:896]
+    most, chunks = bucket(n, starts, cell, w, bcol, bdep, bw, btile)
     count[0] = n
     count[1] = most
     count[2] = chunks
@@ -576,14 +585,14 @@
         compiler_params=comm_params(2, 60 << 20),
     )(ray_counts, tile_brick.T, times, cell_offsets, cell_depths, seg_lengths)
     entries = [shape((PLACES, SEG), d) for d in (i32, f32)] + [shape((BLOCKS, ROWS, 128), d) for d in (i32, i32, f32, i32)]
-    q0, p_part, *lists, info, count = pl.pallas_call(
+    q0, p_part, times, *lists, info, count = pl.pallas_call(
         first_kernel,
-        out_shape=(shape((COLS, DEP)), shape((RAYS + 8, NDEV)), *entries, shape((2, SLOTS), i32), shape((3,), i32)),
-        in_specs=[VMEM],
-        out_specs=(VMEM,) * 9 + (SMEM,),
-        scratch_shapes=SCRATCH,
+        out_shape=(shape((COLS, DEP)), shape((RAYS + 8, NDEV)), shape((1, RAYS)), *entries, shape((2, SLOTS), i32), shape((3,), i32)),
+        in_specs=[VMEM] * 2,
+        out_specs=(VMEM,) * 10 + (SMEM,),
+        scratch_shapes=SCRATCH + [pltpu.VMEM((PLACES, 128), f32)],
         compiler_params=PARAMS,
-    )(held)
+    )(held, times)
     p0, shift, smooth = pl.pallas_call(
         middle_kernel,
         out_shape=(shape((RAYS, NDEV)), shape((8, NDEV)), shape((COLS, DEP))),

time: 85.5 us -> 80.9 us (0.946)
  Pallas kernels: 80.9 us -> 76.9 us
    pallas_call x1, Pallas kernels: 23.1 us -> 20.4 us  [shards(): pl.pallas_call(last_kernel, out_shape=(shape((COLS, DEP)), shape((1, RAYS...]
    pallas_call x1, Pallas kernels: 10.1 us -> 8.27 us  [shards(): pl.pallas_call(first_kernel, out_shape=(shape((COLS, DEP)), shape((RAYS +...]
where the time goes in v7:
time: 80.9 us; the launch traced here: 80.5 us
  Pallas kernels  76.9 us (95%)
  local copies, waits for them, and re-layouts  2.35 us (3%)
  between operations  1.33 us (2%)
    pallas_call x1, Pallas kernels, shards(): pl.pallas_call(send_kernel, out_shape=shape((NDEV, 5, SEG)), in_specs=[SM...  22.9 us
    pallas_call x1, Pallas kernels, shards(): pl.pallas_call(last_kernel, out_shape=(shape((COLS, DEP)), shape((1, RAYS...  20.4 us
    pallas_call x1, Pallas kernels, shards(): pl.pallas_call(middle_kernel, out_shape=(shape((RAYS, NDEV)), shape((8, N...  19.2 us
    pallas_call x1, Pallas kernels, shards(): pl.pallas_call(first_kernel, out_shape=(shape((COLS, DEP)), shape((RAYS +...  8.27 us
    pallas_call x1, Pallas kernels, shards(): pl.pallas_call(second_kernel, out_shape=(shape((COLS, DEP)), shape((RAYS,...  6.11 us
    unnamed x6, local copies, waits for them, and re-layouts  2.35 us

profile of v7, /device:TPU:1, one launch (start us, length us, event | category | flops | bytes accessed | tf_op | source)
XLA Modules:
  0.0 80.5 jit_solution(10833862641088978687)
XLA Ops:
  1.3 0.0 copy-start.1
  1.3 22.9 %shard_map.77.held = f32[128,5,128]{2,1,0:T(8,128)} custom-call(s32[1]{0:T(128)S(6)} %copy.10.count, s32[4,32]{1,0:T(4,128)} %bitcast.8, f32[1,32]{1,0:T(1,128)} %bitcast.5, s32[32,4,128]{2,1,0:T(4,128)} %offs_in.1, s32[32,4,128]{2,1,0:T(4,128)} %deps_in.1, f32[32,4,128]{2,1,0:T(4,128)} %lens_in.1), custom_call_target="tpu_custom_call" | custom-call | tf_op jit(solution)/shard_map/pallas_call | solution.py:577
  24.2 0.0 copy-done.1
  24.2 0.0 copy-start
  24.2 1.0 %copy-done = f32[128,5,128]{2,1,0:T(8,128)S(1)} copy-done((f32[128,5,128]{2,1,0:T(8,128)S(1)}, f32[128,5,128]{2,1,0:T(8,128)}, u32[]{:S(2)}) %copy-start) | copy-done | bytes 327704
  25.2 8.3 %shard_map.78 = (f32[1024,128]{1,0:T(8,128)S(1)}, f32[40,128]{1,0:T(8,128)S(1)}, f32[1,32]{1,0:T(1,128)S(1)}, s32[288,128]{1,0:T(8,128)S(1)}, f32[288,128]{1,0:T...) custom-call(f32[128,5,128]{2,1,0:T(8,128)S(1)} %copy-done, ...), custom_call_target="tpu_custom_call" | custom-call | tf_op jit(solution)/shard_map/pallas_call | solution.py:588
  33.5 19.2 %shard_map.79 = (f32[32,128]{1,0:T(8,128)S(1)}, f32[8,128]{1,0:T(8,128)S(1)}, f32[1024,128]{1,0:T(8,128)S(1)}) custom-call(f32[40,128]{1,0:T(8,128)S(1)} %get-tuple-element.22.p_part, f32[1024,128]{1,0:T(8,128)S(1)} %get-tuple-element.23.q.q0), custom_call_target="tpu_custom_call" | custom-call | tf_op jit(solution)/shard_map/pallas_call | solution.py:596
  52.7 6.1 %shard_map.80 = (f32[1024,128]{1,0:T(8,128)S(1)}, f32[32,128]{1,0:T(8,128)S(1)}, f32[8,128]{1,0:T(8,128)S(1)}) custom-call(f32[32,128]{1,0:T(8,128)S(1)} %get-tuple-element.24.p.p0, f32[8,128]{1,0:T(8,128)S(1)} %get-tuple-element.25.shift, f32[1024,128]{1,0:T(8,128)S(1)} %get-tuple-element.23.q.q0, f32[1024,128]{1,0:T(8,128)S(1)} %get-tuple-element.26.smooth, ...), custom_call_target="tpu_custom_call" | custom-call | tf_op jit(solution)/shard_map/pallas_call | solution.py:605
  58.8 20.4 %shard_map.81 = (f32[1024,128]{1,0:T(8,128)S(1)}, f32[1,32]{1,0:T(1,128)S(1)}) custom-call(s32[1]{0:T(128)S(6)} %copy.10.count, f32[1,32]{1,0:T(1,128)S(1)} %get-tuple-element.21.times, f32[32,128]{1,0:T(8,128)S(1)} %get-tuple-element.35.p_part, f32[32,128]{1,0:T(8,128)S(1)} %get-tuple-element.24.p.p0, f32[8,128]{1,0:T(8,128)S(1)} %get-tuple-element.25.shift, ...), custom_call_target="tpu_custom_call" | custom-call | tf_op jit(solution)/shard_map/pallas_call | solution.py:613
  79.2 0.8 copy.11
  80.0 0.5 copy.12
Async XLA Ops:
  1.3 22.9 %copy-start.1 = (f32[32]{0:T(128)S(1)}, f32[32]{0:T(128)}, u32[]{:S(2)}) copy-start(f32[32]{0:T(128)} %param.6) | copy-start | bytes 388
  24.2 1.0 %copy-start = (f32[128,5,128]{2,1,0:T(8,128)S(1)}, f32[128,5,128]{2,1,0:T(8,128)}, u32[]{:S(2)}) copy-start(f32[128,5,128]{2,1,0:T(8,128)} %shard_map.77.held) | copy-start | bytes 983044

commit v8 on v7

--- a/solution.py
+++ b/solution.py
@@ -138,7 +138,7 @@
     for load in loads:
         load.start()
     barrier = pltpu.get_barrier_semaphore()
-    lines = [p for axis in range(4) for p in stage_peers(here, (axis,))]
+    lines = [p for group in ((1, 0), (2,), (3,)) for p in stage_peers(here, group)]
     for peer in lines:
         pl.semaphore_signal(barrier, inc=1, device_id=peer, device_id_type=MESH)
     tb = brick[...].astype(f32)
@@ -157,12 +157,11 @@
     pay[:, 0:768] = as_payload(cell, w)
     pay[:, 768:896] = marks.astype(bf16)
     pl.semaphore_wait(barrier, len(lines))
-    for s, axis in enumerate((0, 2, 3)):
+    for s, axis in enumerate((2, 3)):
         peers = stage_peers(here, (axis,))
         for peer in peers:
             pl.semaphore_signal(meet_sem.at[s], inc=1, device_id=peer, device_id_type=MESH)
-        if s < 2:
-            place_rank(s, brick_row, rank_row, live, time_row, ray_row, pay, send)
+        place_rank(s, brick_row, rank_row, live, time_row, ray_row, pay, send)
         pl.semaphore_wait(meet_sem.at[s], len(peers))
     me = flat(here)
 
@@ -581,7 +580,7 @@
         out_specs=VMEM,
         scratch_shapes=[pltpu.VMEM((NDEV, 5, SEG), f32), pltpu.VMEM((128, 896), bf16)]
         + [pltpu.VMEM((RAYS, TPR, SEG), d) for d in (i32, i32, f32)]
-        + [pltpu.SemaphoreType.DMA((3,)), pltpu.SemaphoreType.REGULAR((3,)), pltpu.SemaphoreType.DMA, pltpu.SemaphoreType.DMA],
+        + [pltpu.SemaphoreType.DMA((3,)), pltpu.SemaphoreType.REGULAR((2,)), pltpu.SemaphoreType.DMA, pltpu.SemaphoreType.DMA],
         compiler_params=comm_params(2, 60 << 20),
     )(ray_counts, tile_brick.T, times, cell_offsets, cell_depths, seg_lengths)
     entries = [shape((PLACES, SEG), d) for d in (i32, f32)] + [shape((BLOCKS, ROWS, 128), d) for d in (i32, i32, f32, i32)]

time: 80.9 us -> 82.9 us (1.025)
  Pallas kernels: 76.9 us -> 79.5 us
    pallas_call x1, Pallas kernels: 20.4 us -> 23.4 us  [shards(): pl.pallas_call(last_kernel, out_shape=(shape((COLS, DEP)), shape((1, RAYS...]
    pallas_call x1, Pallas kernels: 22.9 us -> 20.6 us  [shards(): pl.pallas_call(send_kernel, out_shape=shape((NDEV, 5, SEG)), in_specs=[SM...]
    pallas_call x1, Pallas kernels: 19.2 us -> 21.1 us  [shards(): pl.pallas_call(middle_kernel, out_shape=(shape((RAYS, NDEV)), shape((8, N...]
where the time goes in v8:
time: 82.9 us; the launch traced here: 83.2 us
  Pallas kernels  79.5 us (96%)
  local copies, waits for them, and re-layouts  2.35 us (3%)
  between operations  1.33 us (2%)
    pallas_call x1, Pallas kernels, shards(): pl.pallas_call(last_kernel, out_shape=(shape((COLS, DEP)), shape((1, RAYS...  23.4 us
    pallas_call x1, Pallas kernels, shards(): pl.pallas_call(middle_kernel, out_shape=(shape((RAYS, NDEV)), shape((8, N...  21.1 us
    pallas_call x1, Pallas kernels, shards(): pl.pallas_call(send_kernel, out_shape=shape((NDEV, 5, SEG)), in_specs=[SM...  20.6 us
    pallas_call x1, Pallas kernels, shards(): pl.pallas_call(first_kernel, out_shape=(shape((COLS, DEP)), shape((RAYS +...  8.27 us
    pallas_call x1, Pallas kernels, shards(): pl.pallas_call(second_kernel, out_shape=(shape((COLS, DEP)), shape((RAYS,...  6.11 us
    unnamed x6, local copies, waits for them, and re-layouts  2.35 us

profile of v8, /device:TPU:1, one launch (start us, length us, event | category | flops | bytes accessed | tf_op | source)
XLA Modules:
  0.0 83.2 jit_solution(12002128978984591877)
XLA Ops:
  1.3 0.0 copy-start.1
  1.3 20.6 %shard_map.77.held = f32[128,5,128]{2,1,0:T(8,128)} custom-call(s32[1]{0:T(128)S(6)} %copy.10.count, s32[4,32]{1,0:T(4,128)} %bitcast.8, f32[1,32]{1,0:T(1,128)} %bitcast.5, s32[32,4,128]{2,1,0:T(4,128)} %offs_in.1, s32[32,4,128]{2,1,0:T(4,128)} %deps_in.1, f32[32,4,128]{2,1,0:T(4,128)} %lens_in.1), custom_call_target="tpu_custom_call" | custom-call | tf_op jit(solution)/shard_map/pallas_call | solution.py:576
  21.9 0.0 copy-done.1
  21.9 0.0 copy-start
  21.9 1.0 %copy-done = f32[128,5,128]{2,1,0:T(8,128)S(1)} copy-done((f32[128,5,128]{2,1,0:T(8,128)S(1)}, f32[128,5,128]{2,1,0:T(8,128)}, u32[]{:S(2)}) %copy-start) | copy-done | bytes 327704
  23.0 8.3 %shard_map.78 = (f32[1024,128]{1,0:T(8,128)S(1)}, f32[40,128]{1,0:T(8,128)S(1)}, f32[1,32]{1,0:T(1,128)S(1)}, s32[288,128]{1,0:T(8,128)S(1)}, f32[288,128]{1,0:T...) custom-call(f32[128,5,128]{2,1,0:T(8,128)S(1)} %copy-done, ...), custom_call_target="tpu_custom_call" | custom-call | tf_op jit(solution)/shard_map/pallas_call | solution.py:587
  31.2 21.1 %shard_map.79 = (f32[32,128]{1,0:T(8,128)S(1)}, f32[8,128]{1,0:T(8,128)S(1)}, f32[1024,128]{1,0:T(8,128)S(1)}) custom-call(f32[40,128]{1,0:T(8,128)S(1)} %get-tuple-element.22.p_part, f32[1024,128]{1,0:T(8,128)S(1)} %get-tuple-element.23.q.q0), custom_call_target="tpu_custom_call" | custom-call | tf_op jit(solution)/shard_map/pallas_call | solution.py:595
  52.3 6.1 %shard_map.80 = (f32[1024,128]{1,0:T(8,128)S(1)}, f32[32,128]{1,0:T(8,128)S(1)}, f32[8,128]{1,0:T(8,128)S(1)}) custom-call(f32[32,128]{1,0:T(8,128)S(1)} %get-tuple-element.24.p.p0, f32[8,128]{1,0:T(8,128)S(1)} %get-tuple-element.25.shift, f32[1024,128]{1,0:T(8,128)S(1)} %get-tuple-element.23.q.q0, f32[1024,128]{1,0:T(8,128)S(1)} %get-tuple-element.26.smooth, ...), custom_call_target="tpu_custom_call" | custom-call | tf_op jit(solution)/shard_map/pallas_call | solution.py:604
  58.5 23.4 %shard_map.81 = (f32[1024,128]{1,0:T(8,128)S(1)}, f32[1,32]{1,0:T(1,128)S(1)}) custom-call(s32[1]{0:T(128)S(6)} %copy.10.count, f32[1,32]{1,0:T(1,128)S(1)} %get-tuple-element.21.times, f32[32,128]{1,0:T(8,128)S(1)} %get-tuple-element.35.p_part, f32[32,128]{1,0:T(8,128)S(1)} %get-tuple-element.24.p.p0, f32[8,128]{1,0:T(8,128)S(1)} %get-tuple-element.25.shift, ...), custom_call_target="tpu_custom_call" | custom-call | tf_op jit(solution)/shard_map/pallas_call | solution.py:612
  81.9 0.8 copy.11
  82.7 0.5 copy.12
Async XLA Ops:
  1.3 20.6 %copy-start.1 = (f32[32]{0:T(128)S(1)}, f32[32]{0:T(128)}, u32[]{:S(2)}) copy-start(f32[32]{0:T(128)} %param.6) | copy-start | bytes 388
  21.9 1.0 %copy-start = (f32[128,5,128]{2,1,0:T(8,128)S(1)}, f32[128,5,128]{2,1,0:T(8,128)}, u32[]{:S(2)}) copy-start(f32[128,5,128]{2,1,0:T(8,128)} %shard_map.77.held) | copy-start | bytes 983044

commit v9 on v8

--- a/solution.py
+++ b/solution.py
@@ -522,7 +522,7 @@
 def last_kernel(count, times, p_part, p0, shift, dots, q0, e, model, misfit, buf, got, small, small_got, norm, edge, halo,
                 send_sem, recv_sem, small_send, small_recv, face_send, face_recv):
     here = coords()
-    meet([p for group in ROUNDS for p in stage_peers(here, group)])
+    meet([p for group in STAGES for p in stage_peers(here, group)] + ring_peers(here)[2:])
     faces = send_halo(here, e, edge, halo, face_send, face_recv)
     buf[0] = p_part[...]
     first = send_stage(0, here, STAGES[0], buf, got, send_sem, recv_sem)
@@ -539,8 +539,8 @@
     buf[1] = add_stage(0, first, buf, got)
     second = send_stage(1, here, STAGES[1], buf, got, send_sem, recv_sem)
     small[1] = add_stage(0, one, small, small_got)
+    buf[2] = add_stage(1, second, buf, got)
     two = send_stage(1, here, ROUNDS[1], small, small_got, small_send, small_recv)
-    buf[2] = add_stage(1, second, buf, got)
     third = send_stage(2, here, STAGES[2], buf, got, send_sem, recv_sem)
     moments = add_stage(1, two, small, small_got)
     pe = add_stage(2, third, buf, got)

time: 82.9 us -> 81.8 us (0.987)
  Pallas kernels: 79.5 us -> 78.2 us
    pallas_call x1, Pallas kernels: 23.4 us -> 21.8 us  [shards(): pl.pallas_call(last_kernel, out_shape=(shape((COLS, DEP)), shape((1, RAYS...]
where the time goes in v9:
time: 81.8 us
  Pallas kernels  78.2 us (96%)
  local copies, waits for them, and re-layouts  2.35 us (3%)
  between operations  1.33 us (2%)
    pallas_call x1, Pallas kernels, shards(): pl.pallas_call(last_kernel, out_shape=(shape((COLS, DEP)), shape((1, RAYS...  21.8 us
    pallas_call x1, Pallas kernels, shards(): pl.pallas_call(middle_kernel, out_shape=(shape((RAYS, NDEV)), shape((8, N...  21.4 us
    pallas_call x1, Pallas kernels, shards(): pl.pallas_call(send_kernel, out_shape=shape((NDEV, 5, SEG)), in_specs=[SM...  20.6 us
    pallas_call x1, Pallas kernels, shards(): pl.pallas_call(first_kernel, out_shape=(shape((COLS, DEP)), shape((RAYS +...  8.27 us
    pallas_call x1, Pallas kernels, shards(): pl.pallas_call(second_kernel, out_shape=(shape((COLS, DEP)), shape((RAYS,...  6.11 us
    unnamed x6, local copies, waits for them, and re-layouts  2.35 us

profile of v9, /device:TPU:1, one launch (start us, length us, event | category | flops | bytes accessed | tf_op | source)
XLA Modules:
  0.0 81.8 jit_solution(17445960908733033290)
XLA Ops:
  1.3 0.0 copy-start.1
  1.3 20.6 %shard_map.77.held = f32[128,5,128]{2,1,0:T(8,128)} custom-call(s32[1]{0:T(128)S(6)} %copy.10.count, s32[4,32]{1,0:T(4,128)} %bitcast.8, f32[1,32]{1,0:T(1,128)} %bitcast.5, s32[32,4,128]{2,1,0:T(4,128)} %offs_in.1, s32[32,4,128]{2,1,0:T(4,128)} %deps_in.1, f32[32,4,128]{2,1,0:T(4,128)} %lens_in.1), custom_call_target="tpu_custom_call" | custom-call | tf_op jit(solution)/shard_map/pallas_call | solution.py:576
  21.9 0.0 copy-done.1
  21.9 0.0 copy-start
  21.9 1.0 %copy-done = f32[128,5,128]{2,1,0:T(8,128)S(1)} copy-done((f32[128,5,128]{2,1,0:T(8,128)S(1)}, f32[128,5,128]{2,1,0:T(8,128)}, u32[]{:S(2)}) %copy-start) | copy-done | bytes 327704
  23.0 8.3 %shard_map.78 = (f32[1024,128]{1,0:T(8,128)S(1)}, f32[40,128]{1,0:T(8,128)S(1)}, f32[1,32]{1,0:T(1,128)S(1)}, s32[288,128]{1,0:T(8,128)S(1)}, f32[288,128]{1,0:T...) custom-call(f32[128,5,128]{2,1,0:T(8,128)S(1)} %copy-done, ...), custom_call_target="tpu_custom_call" | custom-call | tf_op jit(solution)/shard_map/pallas_call | solution.py:587
  31.2 21.4 %shard_map.79 = (f32[32,128]{1,0:T(8,128)S(1)}, f32[8,128]{1,0:T(8,128)S(1)}, f32[1024,128]{1,0:T(8,128)S(1)}) custom-call(f32[40,128]{1,0:T(8,128)S(1)} %get-tuple-element.22.p_part, f32[1024,128]{1,0:T(8,128)S(1)} %get-tuple-element.23.q.q0), custom_call_target="tpu_custom_call" | custom-call | tf_op jit(solution)/shard_map/pallas_call | solution.py:595
  52.6 6.1 %shard_map.80 = (f32[1024,128]{1,0:T(8,128)S(1)}, f32[32,128]{1,0:T(8,128)S(1)}, f32[8,128]{1,0:T(8,128)S(1)}) custom-call(f32[32,128]{1,0:T(8,128)S(1)} %get-tuple-element.24.p.p0, f32[8,128]{1,0:T(8,128)S(1)} %get-tuple-element.25.shift, f32[1024,128]{1,0:T(8,128)S(1)} %get-tuple-element.23.q.q0, f32[1024,128]{1,0:T(8,128)S(1)} %get-tuple-element.26.smooth, ...), custom_call_target="tpu_custom_call" | custom-call | tf_op jit(solution)/shard_map/pallas_call | solution.py:604
  58.8 21.8 %shard_map.81 = (f32[1024,128]{1,0:T(8,128)S(1)}, f32[1,32]{1,0:T(1,128)S(1)}) custom-call(s32[1]{0:T(128)S(6)} %copy.10.count, f32[1,32]{1,0:T(1,128)S(1)} %get-tuple-element.21.times, f32[32,128]{1,0:T(8,128)S(1)} %get-tuple-element.35.p_part, f32[32,128]{1,0:T(8,128)S(1)} %get-tuple-element.24.p.p0, f32[8,128]{1,0:T(8,128)S(1)} %get-tuple-element.25.shift, ...), custom_call_target="tpu_custom_call" | custom-call | tf_op jit(solution)/shard_map/pallas_call | solution.py:612
  80.5 0.8 copy.11
  81.3 0.5 copy.12
Async XLA Ops:
  1.3 20.6 %copy-start.1 = (f32[32]{0:T(128)S(1)}, f32[32]{0:T(128)}, u32[]{:S(2)}) copy-start(f32[32]{0:T(128)} %param.6) | copy-start | bytes 388
  21.9 1.0 %copy-start = (f32[128,5,128]{2,1,0:T(8,128)S(1)}, f32[128,5,128]{2,1,0:T(8,128)}, u32[]{:S(2)}) copy-start(f32[128,5,128]{2,1,0:T(8,128)} %shard_map.77.held) | copy-start | bytes 983044
